TPU v7x, 32 devices: a whole 2x2x4 slice. The times are simulated.
32 devices in a mesh: dp: 8 (over z, y), mp: 4 (over x, core).
Axes of the slice: x: 2, y: 2, z: 4, core: 2. Of those that a mesh axis runs over, the one named last changes fastest.
Arguments:
- tokens: bfloat16 [32768, 512], P(('dp', 'mp')), may hold values from -6 to 6
- cotangent: bfloat16 [32768, 512], P(('dp', 'mp')), may hold values from -6 to 6
- clip_ids: int32 [32768], P('dp'), may hold values from 15 to 511, as said below
- frame_ids: int32 [32768], P('dp'), may hold values from 0 to 15, as said below
- step: int32 [1], replicated, may hold values from 2 to 20
- w_qkv: float32 [3, 512, 512], P(None, 'dp', 'mp'), may hold values from -0.25 to 0.25
- w_out: float32 [512, 512], P('mp', 'dp'), may hold values from -0.75 to 0.75
- w_up: float32 [512, 2048], P('dp', 'mp'), may hold values from -0.25 to 0.25
- w_down: float32 [2048, 512], P('mp', 'dp'), may hold values from -0.125 to 0.125
- norm_params: float32 [4, 512], replicated, may hold values from -0.9 to 1.45, as said below
- moment_qkv: float32 [3, 512, 512], P(None, 'dp', 'mp'), may hold values from -0.00036621094 to 0.00036621094
- moment_out: float32 [512, 512], P('mp', 'dp'), may hold values from -0.00036621094 to 0.00036621094
- moment_up: float32 [512, 2048], P('dp', 'mp'), may hold values from -0.00036621094 to 0.00036621094
- moment_down: float32 [2048, 512], P('mp', 'dp'), may hold values from -0.00036621094 to 0.00036621094
- moment_norm: float32 [4, 512], replicated, may hold values from -0.0009765625 to 0.0009765625
- square_qkv: float32 [3, 512, 512], P(None, 'dp', 'mp'), may hold values from 1.588423e-08 to 6.353692e-08
- square_out: float32 [512, 512], P('mp', 'dp'), may hold values from 1.588423e-08 to 6.353692e-08
- square_up: float32 [512, 2048], P('dp', 'mp'), may hold values from 1.588423e-08 to 6.353692e-08
- square_down: float32 [2048, 512], P('mp', 'dp'), may hold values from 1.588423e-08 to 6.353692e-08
- square_norm: float32 [4, 512], replicated, may hold values from 1.4295807e-07 to 5.718323e-07
- average_qkv: float32 [3, 512, 512], P(None, 'dp', 'mp'), may hold values from -0.25 to 0.25
- average_out: float32 [512, 512], P('mp', 'dp'), may hold values from -0.75 to 0.75
- average_up: float32 [512, 2048], P('dp', 'mp'), may hold values from -0.25 to 0.25
- average_down: float32 [2048, 512], P('mp', 'dp'), may hold values from -0.125 to 0.125
- average_norm: float32 [4, 512], replicated, may hold values from 0.5 to 1.5
Outputs:
- block_out: bfloat16 [32768, 512], P(('dp', 'mp'))
- grad_tokens: float32 [32768, 512], P(('dp', 'mp'))
- grad_norm: float32 [], replicated
- new_qkv: float32 [3, 512, 512], P(None, 'dp', 'mp')
- new_out: float32 [512, 512], P('mp', 'dp')
- new_up: float32 [512, 2048], P('dp', 'mp')
- new_down: float32 [2048, 512], P('mp', 'dp')
- new_norm: float32 [4, 512], replicated
- new_moment_qkv: float32 [3, 512, 512], P(None, 'dp', 'mp')
- new_moment_out: float32 [512, 512], P('mp', 'dp')
- new_moment_up: float32 [512, 2048], P('dp', 'mp')
- new_moment_down: float32 [2048, 512], P('mp', 'dp')
- new_moment_norm: float32 [4, 512], replicated
- new_square_qkv: float32 [3, 512, 512], P(None, 'dp', 'mp')
- new_square_out: float32 [512, 512], P('mp', 'dp')
- new_square_up: float32 [512, 2048], P('dp', 'mp')
- new_square_down: float32 [2048, 512], P('mp', 'dp')
- new_square_norm: float32 [4, 512], replicated
- copy_qkv: bfloat16 [3, 512, 512], P(None, 'dp', 'mp')
- copy_out: bfloat16 [512, 512], P('mp', 'dp')
- copy_up: bfloat16 [512, 2048], P('dp', 'mp')
- copy_down: bfloat16 [2048, 512], P('mp', 'dp')
- new_average_qkv: float32 [3, 512, 512], P(None, 'dp', 'mp')
- new_average_out: float32 [512, 512], P('mp', 'dp')
- new_average_up: float32 [512, 2048], P('dp', 'mp')
- new_average_down: float32 [2048, 512], P('mp', 'dp')
- new_average_norm: float32 [4, 512], replicated
Inputs may be any that keep to these rules, and one draw needn't show every extreme that they name: `clip_ids`: clips are runs of whole frames of 64 tokens with at most 1024 tokens; no clip crosses a boundary between aligned groups of 4096 tokens, and in every such group some clip has exactly 1024 tokens. A clip's number is the index, among all frames of 64 tokens, of its last frame, so numbers never fall along the tokens. `frame_ids`: A token's frame counts whole frames of 64 tokens from the start of its clip. `norm_params`: rows 0 and 2 are gains near one, rows 1 and 3 biases near zero.
All inputs are finite; a program needn't handle non-finite values.
Results may differ from a plain program's by a relative error of at most 0.02.
Values may be sent and summed in bfloat16 or wider, within the bound.
No kernel may reach another device: no remote copies, remote signals or barrier semaphores. Data moves between devices by JAX's collectives and lax.ppermute only.
A program may use at most 128 MiB of HBM per device.

v0:
```python
import functools

import jax
import jax.numpy as jnp
from jax import lax
from jax.experimental import pallas as pl
from jax.experimental.pallas import tpu as pltpu
from jax.sharding import PartitionSpec as P

HEAD = 64
CLIP = 1024
FRAME = 64

norm_eps = 1e-05
beta_one = 0.9
beta_two = 0.95
adam_eps = 1e-08
clip_limit = 1.0
ema_decay = 0.75

F32 = jnp.float32
BF16 = jnp.bfloat16
BOTH = ("dp", "mp")
VMEM = pltpu.VMEM
MASKED = -1e30
PAIR = 2 * HEAD
TQ = 256
TK = 256
ROWS = 256
FEED_ROWS = 1024


def mm(a, b):
    return lax.dot_general(a, b, (((1,), (0,)), ((), ())), preferred_element_type=F32)


def mm_nt(a, b):
    return lax.dot_general(a, b, (((1,), (1,)), ((), ())), preferred_element_type=F32)


def mm_tn(a, b):
    return lax.dot_general(a, b, (((0,), (0,)), ((), ())), preferred_element_type=F32)


def shape(dims, kind):
    return jax.ShapeDtypeStruct(tuple(dims), kind)


def call(body, outs, smem, ins, far=(), scratch=(), flops=0, moved=0, room=60, loose=(), small=()):
    return pl.pallas_call(
        body,
        out_shape=outs,
        in_specs=[pl.BlockSpec(memory_space=pltpu.SMEM)] * len(smem)
        + [pl.BlockSpec(memory_space=VMEM)] * len(ins)
        + [pl.BlockSpec(memory_space=pl.ANY)] * len(far),
        out_specs=tuple(
            pl.BlockSpec(
                memory_space=pl.ANY if i in loose else pltpu.SMEM if i in small else VMEM
            )
            for i in range(len(outs))
        ),
        scratch_shapes=list(scratch),
        compiler_params=pltpu.CompilerParams(vmem_limit_bytes=room << 20),
        cost_estimate=pl.CostEstimate(
            flops=int(flops), bytes_accessed=int(moved), transcendentals=0
        ),
    )(*smem, *ins, *far)


def rows_at(tile, base=0):
    return pl.ds(pl.multiple_of(base + tile * ROWS, ROWS), ROWS)


def normalize(rows):
    center = rows - jnp.mean(rows, axis=-1, keepdims=True)
    inverse = lax.rsqrt(jnp.mean(center * center, axis=-1, keepdims=True) + norm_eps)
    return center * inverse, inverse


def norm_back(grad, xhat, inverse, gain_row):
    gy = grad * gain_row
    return inverse * (
        gy
        - jnp.mean(gy, axis=-1, keepdims=True)
        - xhat * jnp.mean(gy * xhat, axis=-1, keepdims=True)
    )


def place(spots_ref, far, sems, parts):
    copies = []
    for s in range(32):
        row, col = spots_ref[s] // 4, spots_ref[s] % 4
        for t, (start, wide, whole) in enumerate(parts):
            block = far[s // 4].at[s % 4]
            rows = block.shape[-2]
            at = (
                pl.ds(pl.multiple_of(row * rows, rows), rows),
                pl.ds(pl.multiple_of(col * wide, wide), wide),
            )
            lead = (slice(None),) * (len(block.shape) - 2)
            copies.append(
                pltpu.make_async_copy(
                    block.at[lead + (slice(None), pl.ds(start, wide))],
                    whole.at[lead + at],
                    sems.at[s * len(parts) + t],
                )
            )
    for copy in copies:
        copy.start()
    return copies


def fetch(pairs, sems, start=0):
    copies = [
        pltpu.make_async_copy(far, near, sems.at[start + k]) for k, (far, near) in enumerate(pairs)
    ]
    for copy in copies:
        copy.start()
    return copies


def project_body(fast, first_ref, *refs):
    if fast:
        spots_ref, norm_ref, own_far, halo_far = refs[:4]
        far, refs = refs[4:12], refs[12:]
        qkv_ref, kt_ref, vt_ref, xt_ref, w_ref, own_ref, halo_ref, sems = refs
        copies = place(spots_ref, far, sems, [(0, far[0].shape[-1], w_ref)])
        copies += fetch(((own_far, own_ref), (halo_far, halo_ref)), sems, 32)
        for copy in copies:
            copy.wait()
    else:
        own_ref, halo_ref, norm_ref, w_ref, qkv_ref, kt_ref, vt_ref, xt_ref = refs
    gain, shift = norm_ref[0:1, :], norm_ref[1:2, :]
    pairs = w_ref.shape[1] // (3 * PAIR)

    def rows_of(ref, tile, base):
        to = rows_at(tile, base)
        xhat, _ = normalize(ref[rows_at(tile), :].astype(F32))
        xn = xhat * gain + shift
        xt_ref[:, to] = xn.T.astype(BF16)
        xn = xn.astype(BF16)
        for p in range(pairs):
            at, lanes = p * 3 * PAIR, slice(p * PAIR, (p + 1) * PAIR)
            qkv = mm(xn, w_ref[:, at : at + 3 * PAIR])
            qkv_ref[to, at : at + 3 * PAIR] = qkv.astype(BF16)
            kt_ref[lanes, to] = qkv[:, PAIR : 2 * PAIR].T.astype(BF16)
            vt_ref[lanes, to] = qkv[:, 2 * PAIR :].T.astype(BF16)

    @pl.loop(jnp.minimum(first_ref[0], CLIP // ROWS), CLIP // ROWS)
    def _(tile):
        rows_of(halo_ref, tile, 0)

    @pl.loop(0, own_ref.shape[0] // ROWS)
    def _(tile):
        rows_of(own_ref, tile, CLIP)


def project(first, own, halo, norms, w_qkv, spots=None, far=()):
    n, d = own.shape
    total = n + CLIP
    fast = len(far) > 0
    outs = (
        shape((total, 3 * d), BF16),
        shape((d, total), BF16),
        shape((d, total), BF16),
        shape((d, total), BF16),
    )
    if fast:
        outs += (shape((d, 3 * d), BF16),)
    return call(
        functools.partial(project_body, fast),
        outs,
        (first, spots) if fast else (first,),
        (norms,) if fast else (own, halo, norms, w_qkv),
        (own, halo) + tuple(far) if fast else (),
        (VMEM(own.shape, BF16), VMEM(halo.shape, BF16), pltpu.SemaphoreType.DMA((34,)))
        if fast
        else (),
        flops=6 * d * d * total,
        moved=2 * d * (6 * total + 2 * n) + 6 * d * d,
        room=24,
    )


def split_heads(pair):
    zero = jnp.zeros((HEAD, pair.shape[1]), pair.dtype)
    return jnp.concatenate(
        [
            jnp.concatenate([pair[:HEAD], zero], axis=1),
            jnp.concatenate([zero, pair[HEAD:]], axis=1),
        ]
    )


def twice(row):
    return jnp.concatenate([row, row], axis=1)


def sight(low_ref, at, i):
    spot = lax.broadcasted_iota(jnp.int32, (1, TQ), 1)
    last = ((CLIP + i * TQ) + spot) >> 6
    frame = lax.broadcasted_iota(jnp.int32, (TK, 2 * TQ), 0) >> 6
    return twice(low_ref[0:1, at]), twice(last), frame


def attend_body(
    first_ref, low_ref, qkv_ref, vt_ref, mix_ref, log_ref, qt, acc, top, total, s_ref, p_ref
):
    pairs = mix_ref.shape[1] // PAIR

    @pl.loop(0, mix_ref.shape[0] // TQ)
    def _(i):
        at = pl.ds(pl.multiple_of(i * TQ, TQ), TQ)
        low, last, frame = sight(low_ref, at, i)
        here = pl.ds(pl.multiple_of(CLIP + i * TQ, TQ), TQ)
        for p in range(pairs):
            query = qkv_ref[here, p * 3 * PAIR : (p * 3 + 1) * PAIR] * HEAD**-0.5
            qt[p] = split_heads(query.T)
        acc[...] = jnp.zeros_like(acc)
        top[...] = jnp.full_like(top, MASKED)
        total[...] = jnp.zeros_like(total)

        def step(j, carry):
            keys = pl.ds(pl.multiple_of(j * TK, TK), TK)
            shift = j * (TK // FRAME)
            visible = (frame >= low - shift) & (frame <= last - shift)
            for p in range(pairs):
                scores = mm(qkv_ref[keys, (p * 3 + 1) * PAIR : (p * 3 + 2) * PAIR], qt[p])
                s_ref[p] = jnp.where(visible, scores, MASKED)
            for p in range(pairs):
                scores = s_ref[p]
                old = top[p]
                new = jnp.maximum(old, jnp.max(scores, axis=0, keepdims=True))
                weights = jnp.exp(scores - new)
                keep = jnp.exp(old - new)
                top[p] = new
                total[p] = total[p] * keep + jnp.sum(weights, axis=0, keepdims=True)
                p_ref[p] = weights.astype(BF16)
                for h in range(2):
                    part = slice(h * HEAD, (h + 1) * HEAD)
                    acc[p, part, :] = acc[p, part, :] * keep[:, h * TQ : (h + 1) * TQ]
            for p in range(pairs):
                for h in range(2):
                    part = slice(h * HEAD, (h + 1) * HEAD)
                    values = vt_ref[p * PAIR + h * HEAD : p * PAIR + (h + 1) * HEAD, keys]
                    acc[p, part, :] += mm(values, p_ref[p, :, h * TQ : (h + 1) * TQ])
            return carry

        lax.fori_loop(first_ref[i], (CLIP + (i + 1) * TQ + TK - 1) // TK, step, 0)
        for p in range(pairs):
            sums = total[p]
            logs = top[p] + jnp.log(sums)
            inverse = 1.0 / sums
            for h in range(2):
                part = slice(h * HEAD, (h + 1) * HEAD)
                wide = slice(h * TQ, (h + 1) * TQ)
                acc[p, part, :] = acc[p, part, :] * inverse[:, wide]
                log_ref[2 * p + h : 2 * p + h + 1, at] = logs[:, wide]
            mix_ref[at, p * PAIR : (p + 1) * PAIR] = acc[p].T.astype(BF16)


def attend(first, low, qkv, vt):
    d, total = vt.shape
    n = total - CLIP
    pairs = d // PAIR
    return call(
        attend_body,
        (shape((n, d), BF16), shape((d // HEAD, n), F32)),
        (first,),
        (low, qkv, vt),
        scratch=(
            VMEM((pairs, PAIR, 2 * TQ), BF16),
            VMEM((pairs, PAIR, TQ), F32),
            VMEM((pairs, 1, 2 * TQ), F32),
            VMEM((pairs, 1, 2 * TQ), F32),
            VMEM((pairs, TK, 2 * TQ), F32),
            VMEM((pairs, TK, 2 * TQ), BF16),
        ),
        flops=16 * n * 1024 * d,
        moved=2 * d * (2 * n + 4 * total),
        room=24,
    )


def attend_back_body(fast, first_ref, *refs):
    if fast:
        slots_ref, side_ref, refs = refs[0], refs[1], refs[2:]
    low_ref, qkv_ref, kt_ref, xt_ref, mix_ref, log_ref, grad_ref, gt_ref = refs[:8]
    outs, refs = refs[8 : 10 if fast else 9], refs[10 if fast else 9 :]
    qt, gt, qs, gs, acc, dk_acc, dv_acc, s_ref, d_ref, p_ref, ds_ref, rows_ref, g_acc = refs
    n, d = grad_ref.shape
    pairs = d // PAIR
    start = jnp.minimum(first_ref[0], CLIP // ROWS)
    tiles = qkv_ref.shape[0] // ROWS

    @pl.loop(start, tiles)
    def _(tile):
        dk_acc[:, rows_at(tile)] = jnp.zeros((d, ROWS), F32)
        dv_acc[:, rows_at(tile)] = jnp.zeros((d, ROWS), F32)

    @pl.loop(start, CLIP // ROWS)
    def _(tile):
        for p in range(pairs):
            gt_ref[p * 3 * PAIR : (p * 3 + 1) * PAIR, rows_at(tile)] = jnp.zeros((PAIR, ROWS), BF16)

    @pl.loop(0, n // TQ)
    def _(i):
        at = pl.ds(pl.multiple_of(i * TQ, TQ), TQ)
        here = pl.ds(pl.multiple_of(CLIP + i * TQ, TQ), TQ)
        low, last, frame = sight(low_ref, at, i)
        for p in range(pairs):
            lanes = slice(p * PAIR, (p + 1) * PAIR)
            query = (qkv_ref[here, p * 3 * PAIR : (p * 3 + 1) * PAIR] * HEAD**-0.5).T
            grad = grad_ref[at, lanes]
            both = (grad.astype(F32) * mix_ref[at, lanes].astype(F32)).T
            grad = grad.T
            qt[p] = query
            gt[p] = grad
            qs[p] = split_heads(query)
            gs[p] = split_heads(grad)
            for h in range(2):
                wide = slice(h * TQ, (h + 1) * TQ)
                rows_ref[p, 0:1, wide] = jnp.sum(
                    both[h * HEAD : (h + 1) * HEAD], axis=0, keepdims=True
                )
                rows_ref[p, 1:2, wide] = log_ref[2 * p + h : 2 * p + h + 1, at]
        acc[...] = jnp.zeros_like(acc)

        def step(j, carry):
            keys = pl.ds(pl.multiple_of(j * TK, TK), TK)
            shift = j * (TK // FRAME)
            visible = (frame >= low - shift) & (frame <= last - shift)
            for p in range(pairs):
                one = (p * 3 + 1) * PAIR
                scores = mm(qkv_ref[keys, one : one + PAIR], qs[p])
                s_ref[p] = jnp.where(visible, scores, MASKED)
                d_ref[p] = mm(qkv_ref[keys, one + PAIR : one + 2 * PAIR], gs[p])
            for p in range(pairs):
                probs = jnp.exp(s_ref[p] - rows_ref[p, 1:2, :])
                p_ref[p] = probs.astype(BF16)
                ds_ref[p] = (probs * (d_ref[p] - rows_ref[p, 0:1, :])).astype(BF16)
            for p in range(pairs):
                for h in range(2):
                    part = slice(h * HEAD, (h + 1) * HEAD)
                    rows = slice(p * PAIR + h * HEAD, p * PAIR + (h + 1) * HEAD)
                    wide = slice(h * TQ, (h + 1) * TQ)
                    dv_acc[rows, keys] += mm_nt(gt[p, part, :], p_ref[p, :, wide])
                    dk_acc[rows, keys] += mm_nt(qt[p, part, :], ds_ref[p, :, wide])
                    acc[p, part, :] += mm(kt_ref[rows, keys], ds_ref[p, :, wide])
            return carry

        lax.fori_loop(first_ref[i], (CLIP + (i + 1) * TQ + TK - 1) // TK, step, 0)
        for p in range(pairs):
            gt_ref[p * 3 * PAIR : (p * 3 + 1) * PAIR, here] = (acc[p] * HEAD**-0.5).astype(BF16)

    @pl.loop(start, tiles)
    def _(tile):
        at = rows_at(tile)
        for p in range(pairs):
            one, rows = (p * 3 + 1) * PAIR, slice(p * PAIR, (p + 1) * PAIR)
            gt_ref[one : one + PAIR, at] = dk_acc[rows, at].astype(BF16)
            gt_ref[one + PAIR : one + 2 * PAIR, at] = dv_acc[rows, at].astype(BF16)

    wide = 6 * PAIR

    def weights(side):
        rows = pl.ds(pl.multiple_of(side * wide, wide), wide)
        g_acc[...] = mm_nt(xt_ref[:, CLIP:], gt_ref[rows, CLIP:])

        @pl.loop(start, CLIP // ROWS)
        def _(tile):
            g_acc[...] += mm_nt(xt_ref[:, rows_at(tile)], gt_ref[rows, rows_at(tile)])

    if not fast:
        for side in range(d // (2 * PAIR)):
            weights(side)
            outs[0][:, side * wide : (side + 1) * wide] = g_acc[...].astype(BF16)
        return
    rows = d // 8
    for k in range(2):
        side = side_ref[k]
        weights(side)
        for x in range(2):
            for r in range(8):
                slot = slots_ref[r * 4 + side * 2 + x] & 15
                outs[k][slot] = g_acc[
                    r * rows : (r + 1) * rows, x * 3 * PAIR : (x + 1) * 3 * PAIR
                ].astype(BF16)


def attend_back(first, low, qkv, kt, xt, mixture, logs, grad, slots=None, side=None):
    n, d = grad.shape
    total = qkv.shape[0]
    pairs = d // PAIR
    fast = slots is not None
    outs = (shape((3 * d, total), BF16),)
    if fast:
        outs += (shape((16, d // 8, 3 * d // 4), BF16),) * 2
    else:
        outs += (shape((d, 3 * d), BF16),)
    return call(
        functools.partial(attend_back_body, fast),
        outs,
        (first, slots, side) if fast else (first,),
        (low, qkv, kt, xt, mixture, logs, grad),
        scratch=(
            VMEM((pairs, PAIR, TQ), BF16),
            VMEM((pairs, PAIR, TQ), BF16),
            VMEM((pairs, PAIR, 2 * TQ), BF16),
            VMEM((pairs, PAIR, 2 * TQ), BF16),
            VMEM((pairs, PAIR, TQ), F32),
            VMEM((d, total), F32),
            VMEM((d, total), F32),
            VMEM((pairs, TK, 2 * TQ), F32),
            VMEM((pairs, TK, 2 * TQ), F32),
            VMEM((pairs, TK, 2 * TQ), BF16),
            VMEM((pairs, TK, 2 * TQ), BF16),
            VMEM((pairs, 8, 2 * TQ), F32),
            VMEM((d, 6 * PAIR), F32),
        ),
        flops=40 * n * 1024 * d,
        moved=2 * d * (2 * n + 8 * total),
        room=38,
    )


def chunks_of(far, near, size):
    return [
        (far.at[pl.ds(i, size), :], near.at[pl.ds(i, size), :])
        for i in range(0, near.shape[0], size)
    ]


def feed_blocks(slots_ref, side, mix_ref, act_ref, gh_ref, n2t_ref, lowt_ref, cott_ref, out_ref):
    d = n2t_ref.shape[0]
    one, wide, rows = d // 4, act_ref.shape[1] // 2, d // 8
    small = pl.ds(pl.multiple_of(side * 2 * one, 2 * one), 2 * one)
    spots = [[slots_ref[r * 4 + side * 2 + x] & 15 for r in range(8)] for x in range(2)]
    for start, size, left, right in (
        (0, one, lowt_ref, mix_ref[:, small]),
        (one, wide, n2t_ref, gh_ref),
        (one + wide, wide, cott_ref, act_ref),
    ):
        for x in range(2):
            grad = mm(left[...], right[:, x * size : (x + 1) * size]).astype(BF16)
            for r in range(8):
                out_ref[spots[x][r], :, start : start + size] = grad[r * rows : (r + 1) * rows]


def feed_kept_body(slots_ref, side_ref, *refs):
    feed_blocks(slots_ref, side_ref[0], *refs)


def feed_kept(slots, side, mixture, act, gh, n2t, lowt, cott):
    n, half = act.shape
    d = n2t.shape[0]
    return call(
        feed_kept_body,
        (shape((16, d // 8, d // 4 + half), BF16),),
        (slots, side),
        (mixture, act, gh, n2t, lowt, cott),
        flops=n * d * (4 * half + d),
        moved=2 * n * (4 * d + 2 * half),
        room=20,
    )[0]


def feed_body(fast, *refs):
    late = []
    if fast:
        spots_ref, slots_ref, side_ref, mix_ref, norm_ref, x_far, cot_far = refs[:7]
        far, refs = refs[7:15], refs[15:]
        out_ref, gmix_ref, gmid_ref, gain_ref, sent_ref, act_kept, gh_kept = refs[:7]
        (n2t_ref, lowt_ref, cott_ref), refs = refs[7:10], refs[10:]
        wo_ref, up_ref, down_ref, x_ref, cot_ref, sems, act_sent, gh_sent = refs
        acts, ghs = (act_kept, act_sent), (gh_kept, gh_sent)
        one, ff = wo_ref.shape[1] // 4, up_ref.shape[1] // 4
        near = fetch(chunks_of(x_far, x_ref, 256) + chunks_of(cot_far, cot_ref, 256), sems, 96)
        copies = place(
            spots_ref, far, sems,
            [(0, one, wo_ref), (one, ff, up_ref), (one + ff, ff, down_ref)],
        )
        late = [copy for k, copy in enumerate(copies) if k % 3]
        for copy in near + copies[::3]:
            copy.wait()
    else:
        x_ref, mix_ref, cot_ref, norm_ref, wo_ref, up_ref, down_ref = refs[:7]
        out_ref, gmix_ref, gmid_ref, gain_ref = refs[7:11]
        outs, refs = refs[11:14], refs[14:]
        act_ref, gh_ref, n2t_ref, lowt_ref, cott_ref = refs
        acts, ghs = (act_ref,), (gh_ref,)
    gain, shift = norm_ref[2:3, :], norm_ref[3:4, :]
    ff = up_ref.shape[1]
    d = x_ref.shape[1]
    wide = min(512, ff)
    held = acts[0].shape[1]
    root = 0.7978845608028654
    gain_ref[...] = jnp.zeros_like(gain_ref)
    rows = min(FEED_ROWS, x_ref.shape[0])

    @pl.loop(0, x_ref.shape[0] // rows)
    def _(tile):
        at = pl.ds(pl.multiple_of(tile * rows, rows), rows)
        cot = cot_ref[at, :]
        cott_ref[:, at] = cot.T
        middle = x_ref[at, :].astype(F32) + mm_nt(mix_ref[at, :], wo_ref[...])
        xhat, inverse = normalize(middle)
        n2 = xhat * gain + shift
        n2t_ref[:, at] = n2.T.astype(BF16)
        n2 = n2.astype(BF16)
        if late:

            @pl.when(tile == 0)
            def _():
                for copy in late:
                    copy.wait()

        out = middle
        second = jnp.zeros_like(middle)
        for k in range(len(acts)):
            base = side_ref[k] * held if fast else 0
            for c in range(held // wide):
                cols = pl.ds(pl.multiple_of(base + c * wide, wide), wide)
                to = slice(c * wide, (c + 1) * wide)
                hidden = mm(n2, up_ref[:, cols])
                square = hidden * hidden
                bent = jnp.tanh(hidden * (root + (root * 0.044715) * square))
                half = 0.5 + 0.5 * bent
                active = (hidden * half).astype(BF16)
                slope = half + hidden * (1.0 - bent * bent) * (
                    0.5 * root + (0.5 * root * 3 * 0.044715) * square
                )
                acts[k][at, to] = active
                out += mm_nt(active, down_ref[:, cols])
                gh = (mm(cot, down_ref[:, cols]) * slope).astype(BF16)
                ghs[k][at, to] = gh
                second += mm_nt(gh, up_ref[:, cols])
        out_ref[at, :] = out.astype(BF16)
        gain_ref[0:1, :] += jnp.sum(second * xhat, axis=0, keepdims=True)
        gain_ref[1:2, :] += jnp.sum(second, axis=0, keepdims=True)
        gmid = cot.astype(F32) + norm_back(second, xhat, inverse, gain)
        gmid_ref[at, :] = gmid
        lowt_ref[:, at] = gmid.T.astype(BF16)
        gmix_ref[at, :] = mm(gmid.astype(BF16), wo_ref[...]).astype(BF16)

    if fast:
        feed_blocks(
            slots_ref, side_ref[1], mix_ref, acts[1], ghs[1], n2t_ref, lowt_ref, cott_ref, sent_ref
        )
        return
    gup_ref, gdown_ref, gout_ref = outs
    for c in range(ff // wide):
        cols = slice(c * wide, (c + 1) * wide)
        gup_ref[:, cols] = mm(n2t_ref[...], gh_ref[:, cols]).astype(BF16)
        gdown_ref[:, cols] = mm(cott_ref[...], act_ref[:, cols]).astype(BF16)
    gout_ref[...] = mm(lowt_ref[...], mix_ref[...]).astype(BF16)


def feed(x, mixture, cot, norms, full, ff, spots=None, slots=None, side=None, far=()):
    n, d = x.shape
    fast = len(far) > 0
    outs = (shape((n, d), BF16), shape((n, d), BF16), shape((n, d), F32), shape((2, d), F32))
    turned = (shape((d, n), BF16),) * 3
    if fast:
        outs += (shape((16, d // 8, d // 4 + ff // 2), BF16),)
        outs += (shape((n, ff // 2), BF16),) * 2 + turned
        scratch = (
            VMEM((d, d), BF16),
            VMEM((d, ff), BF16),
            VMEM((d, ff), BF16),
            VMEM((n, d), BF16),
            VMEM((n, d), BF16),
            pltpu.SemaphoreType.DMA((96 + 2 * (n // 256),)),
            VMEM((n, ff // 2), BF16),
            VMEM((n, ff // 2), BF16),
        )
    else:
        outs += (shape((d, ff), BF16), shape((d, ff), BF16), shape((d, d), BF16))
        scratch = (VMEM((n, ff), BF16),) * 2 + tuple(VMEM(t.shape, BF16) for t in turned)
    return call(
        functools.partial(feed_body, fast),
        outs,
        (spots, slots, side) if fast else (),
        (mixture, norms) if fast else (x, mixture, cot, norms) + tuple(full),
        (x, cot) + tuple(far) if fast else (),
        scratch,
        flops=2 * n * d * (6 * ff + 3 * d),
        moved=2 * n * 6 * d + 8 * d * ff,
        room=34,
    )


def first_back_body(
    first_ref, norm_ref, w_ref, gmid_ref, gt_ref, own_far, halo_far, grad_ref, back_ref, gain_ref,
    own_ref, halo_ref, sems,
):
    for copy in fetch(((own_far, own_ref), (halo_far, halo_ref)), sems):
        copy.wait()
    gain = norm_ref[0:1, :]
    gain_ref[...] = jnp.zeros_like(gain_ref)
    start = jnp.minimum(first_ref[0], CLIP // ROWS)

    def rows_of(ref, tile, base, own):
        at = rows_at(tile)
        first = mm(w_ref[...], gt_ref[:, rows_at(tile, base)]).T
        xhat, inverse = normalize(ref[at, :].astype(F32))
        gain_ref[0:1, :] += jnp.sum(first * xhat, axis=0, keepdims=True)
        gain_ref[1:2, :] += jnp.sum(first, axis=0, keepdims=True)
        grad = norm_back(first, xhat, inverse, gain)
        if own:
            grad_ref[at, :] = gmid_ref[at, :] + grad
        else:
            back_ref[at, :] = grad.astype(BF16)

    @pl.loop(0, start)
    def _(tile):
        back_ref[rows_at(tile), :] = jnp.zeros((ROWS, back_ref.shape[1]), BF16)

    @pl.loop(start, CLIP // ROWS)
    def _(tile):
        rows_of(halo_ref, tile, 0, False)

    @pl.loop(0, own_ref.shape[0] // ROWS)
    def _(tile):
        rows_of(own_ref, tile, CLIP, True)


def first_back(first, own, halo, norms, w_qkv, gmid, gt):
    n, d = own.shape
    total = n + CLIP
    return call(
        first_back_body,
        (shape((n, d), F32), shape((CLIP, d), BF16), shape((2, d), F32)),
        (first,),
        (norms, w_qkv, gmid, gt),
        (own, halo),
        (VMEM(own.shape, BF16), VMEM(halo.shape, BF16), pltpu.SemaphoreType.DMA((2,))),
        flops=6 * d * d * total,
        moved=2 * d * (4 * total + 6 * n),
        room=24,
    )


class Grid:
    def __init__(self, dp, mp):
        self.dp, self.mp = dp, mp
        self.fast = (dp, mp) == (8, 4)

    def swap(self, value, z=0, y=0, x=0, c=0):
        bits = z * 8 + y * 4 + x * 2 + c
        return lax.ppermute(value, BOTH, [(i, i ^ bits) for i in range(self.dp * self.mp)])

    def spot(self):
        dp, mp = lax.axis_index("dp"), lax.axis_index("mp")
        return dp // 2, dp % 2, mp // 2, mp % 2

    def slots(self):
        z, y, x, c = self.spot()
        s = jnp.arange(32, dtype=jnp.int32)
        oz, oy, oc, ox = s >> 3, (s >> 2) & 1, (s >> 1) & 1, s & 1
        return (oc ^ c) * 16 + (ox ^ x) * 8 + (oy ^ y) * 4 + (oz ^ z)

    def spots(self):
        z, y, x, c = self.spot()
        s = jnp.arange(32, dtype=jnp.int32)
        oc, ox, oy, oz = (s >> 4) ^ c, ((s >> 3) & 1) ^ x, ((s >> 2) & 1) ^ y, (s & 3) ^ z
        return ((oz * 2 + oy) * 2 + oc) * 2 + ox

    def sides(self):
        c = lax.axis_index("mp") % 2
        return jnp.stack([c, 1 - c]).astype(jnp.int32)

    def gather_z(self, block):
        return jnp.stack([block] + [self.swap(block, z=k) for k in (1, 2, 3)])

    def across(self, held):
        return tuple(self.swap(a, c=1) for a in held)

    def gather_plane(self, near):
        return near, self.swap(near, y=1), self.swap(near, x=1), self.swap(near, y=1, x=1)

    def scatter_core(self, sent):
        return self.swap(sent, c=1)

    def scatter_plane(self, kept, got):
        own, one, two, three = (added(kept[k : k + 4], got[k : k + 4]) for k in (0, 4, 8, 12))
        return own, self.swap(one, y=1), self.swap(two, x=1), self.swap(three, y=1, x=1)

    def scatter_z(self, held):
        parts = [sum(a[k].astype(F32) for a in held).astype(BF16) for k in range(4)]
        return [parts[0]] + [self.swap(parts[k], z=k) for k in (1, 2, 3)]


def added(a, b):
    return (a.astype(F32) + b.astype(F32)).astype(BF16)


def whole_of(block):
    m = block.ndim - 2
    half = lax.all_gather(block, "dp", axis=m, tiled=True)
    return lax.all_gather(half, "mp", axis=m + 1, tiled=True)


def share_of(whole):
    m = whole.ndim - 2
    half = lax.psum_scatter(whole, "mp", scatter_dimension=m + 1, tiled=True)
    return lax.psum_scatter(half, "dp", scatter_dimension=m, tiled=True).astype(F32)


def beside(whole):
    d = whole.shape[1]
    return whole.reshape(3, d, d // PAIR, PAIR).transpose(1, 2, 0, 3).reshape(d, 3 * d)


def apart(wide):
    d = wide.shape[0]
    return wide.reshape(d, d // PAIR, 3, PAIR).transpose(2, 0, 1, 3).reshape(3, d, d)


def after(value, *others):
    return lax.optimization_barrier((value,) + others)[0]


def in_hbm(value):
    return pltpu.with_memory_space_constraint(value, pltpu.HBM)


def joined(*values):
    return lax.optimization_barrier(values)


def adam_update(
    weight, gradient, moment, square, average, step_rate, decay_rate, factor, fixed_one, fixed_two
):
    gradient = gradient * factor
    moment = beta_one * moment + (1.0 - beta_one) * gradient
    square = beta_two * square + (1.0 - beta_two) * gradient * gradient
    weight = weight - step_rate * (
        moment / fixed_one / (jnp.sqrt(square / fixed_two) + adam_eps) + decay_rate * weight
    )
    average = ema_decay * average + (1.0 - ema_decay) * weight
    return (weight, moment, square, average)


RATES = ((0.03, 0.1), (0.09, 0.1), (0.03, 0.1), (0.015, 0.1), (0.2, 0.0))


def total_body(*refs):
    rest, qkv, (one_ref, two_ref) = refs[:4], refs[4:8], refs[8:10]
    out_ref, up_ref, down_ref, qkv_ref, sums_ref = refs[10:]
    small, wide = out_ref.shape[1], up_ref.shape[1]
    width = sums_ref.shape[1]

    def sum_of(parts, at, size):
        a, b, c, d = (p[:, at : at + size].astype(F32) for p in parts)
        return (a + b) + (c + d)

    def squares(value):
        row = jnp.sum(value * value, axis=0, keepdims=True)
        return row if row.shape[1] == width else jnp.concatenate([row] + [jnp.zeros_like(row)] * (width // row.shape[1] - 1), axis=1)

    grad = sum_of(rest, 0, small)
    out_ref[...] = grad
    square = squares(grad)
    for ref, at in ((up_ref, small), (down_ref, small + wide)):
        grad = sum_of(rest, at, wide)
        ref[...] = grad
        square += squares(grad)
    for k in range(3):
        grad = sum_of(qkv, k * PAIR, PAIR)
        qkv_ref[k] = grad
        square += squares(grad)
    sums_ref[...] = jnp.zeros_like(sums_ref)
    sums_ref[0:2, :] = one_ref[...]
    sums_ref[2:4, :] = two_ref[...]
    sums_ref[4:5, :] = square


def totals(rest, qkv, gains_one, gains_two):
    rows, wide = rest[0].shape
    small = qkv[0].shape[1] // 3
    wide = (wide - small) // 2
    return call(
        total_body,
        (
            shape((rows, small), F32),
            shape((rows, wide), F32),
            shape((rows, wide), F32),
            shape((3, rows, small), F32),
            shape((8, gains_one.shape[1]), F32),
        ),
        (),
        tuple(rest) + tuple(qkv) + (gains_one, gains_two),
        moved=12 * rest[0].size,
        room=16,
    )


def adam_body(parts, scale_ref, *refs):
    sums, grads, refs = refs[:parts], refs[parts : parts + 4], refs[parts + 4 :]
    far, outs, norm_ref, held, sems = refs[:20], refs[20:44], refs[44], refs[45:65], refs[65]
    copies = fetch(tuple(zip(far, held)), sems)
    total = sums[0][...]
    if parts == 4:
        total = (total + sums[1][...]) + (sums[2][...] + sums[3][...])
    gains = total[0:4]
    square = jnp.sum(total[4:5]) + jnp.sum(gains * gains)
    norm = jnp.sqrt(jnp.broadcast_to(square, (1, 1)))
    norm_ref[0, 0] = jnp.sum(norm)
    factor = jnp.minimum(1.0, clip_limit / (norm + 1e-06))
    fixed_one, fixed_two = scale_ref[0], scale_ref[1]
    for copy in copies:
        copy.wait()
    for k, (rate, decay) in enumerate(RATES):
        weight, moment, square, average = (ref[...] for ref in held[4 * k : 4 * k + 4])
        grad = grads[k][...] if k < 4 else gains
        new = adam_update(
            weight, grad, moment, square, average, rate, decay, factor, fixed_one, fixed_two
        )
        for i in range(4):
            outs[4 * k + i][...] = new[i]
        if k < 4:
            outs[20 + k][...] = new[0].astype(BF16)


def adam(sums, scales, grads, sets):
    outs = tuple(shape(s[0].shape, F32) for s in sets for _ in range(4))
    outs += tuple(shape(s[0].shape, BF16) for s in sets[:4]) + (shape((1, 1), F32),)
    got = call(
        functools.partial(adam_body, len(sums)),
        outs,
        (scales,),
        tuple(sums) + tuple(grads),
        sum((tuple(s) for s in sets), ()),
        tuple(VMEM(a.shape, F32) for s in sets for a in s) + (pltpu.SemaphoreType.DMA((20,)),),
        flops=30 * sum(s[0].size for s in sets),
        moved=38 * sum(s[0].size for s in sets),
        room=16,
        small=(24,),
    )
    return [got[4 * k : 4 * k + 4] for k in range(5)], got[20:24], got[24]


def per_device(
    grid,
    tokens,
    cotangent,
    clip_ids,
    frame_ids,
    step,
    w_qkv,
    w_out,
    w_up,
    w_down,
    norm_params,
    moment_qkv,
    moment_out,
    moment_up,
    moment_down,
    moment_norm,
    square_qkv,
    square_out,
    square_up,
    square_down,
    square_norm,
    average_qkv,
    average_out,
    average_up,
    average_down,
    average_norm,
):
    n, d = tokens.shape
    back_steps = CLIP // n
    mp_index = lax.axis_index("mp")

    def shifted(value, k):
        pairs = [(i, i + k) for i in range(grid.mp) if 0 <= i + k < grid.mp]
        return lax.ppermute(value, "mp", pairs)

    frames = lax.dynamic_slice_in_dim(frame_ids, mp_index * n, n, 0)
    low = (CLIP + jnp.arange(n, dtype=jnp.int32)) // FRAME - frames
    first = low[::TQ] * FRAME // TK
    low = low.reshape(1, n)

    low_qkv, low_out, low_up, low_down = (
        jnp.concatenate([w_qkv[0], w_qkv[1], w_qkv[2]], axis=1).astype(BF16)
        if grid.fast
        else w_qkv.astype(BF16),
        w_out.T.astype(BF16),
        w_up.astype(BF16),
        w_down.T.astype(BF16),
    )
    if grid.fast:
        slots, spots, side = grid.slots(), grid.spots(), grid.sides()
        rest = jnp.concatenate([low_out, low_up, low_down], axis=1)
        near, halo = joined(grid.gather_z(low_qkv), shifted(tokens, 1))
        rest = after(rest, near)
        near_rest = grid.gather_z(rest)
        near_rest, *held = joined(near_rest, *grid.gather_plane(near))
        far = tuple(held) + grid.across(held)
        held = grid.gather_plane(near_rest)
        qkv, kt, vt, xt, full_qkv = project(first, tokens, halo, norm_params, None, spots, far)
        mixture, logs = attend(first, low, qkv, vt)
        mixture, *held = joined(mixture, *held)
        far = tuple(held) + grid.across(held)
        block_out, gmix, gmid, gains_two, sent, *parts = feed(
            in_hbm(tokens), mixture, in_hbm(cotangent), norm_params, None, 4 * low_up.shape[1],
            spots, slots, side, far,
        )
        kept = feed_kept(slots, side, mixture, *parts)
        got, gmix, kept = joined(grid.scatter_core(sent), gmix, kept)
        held = grid.scatter_plane(kept, got)
        gt, kept_qkv, sent = attend_back(
            first, low, qkv, kt, xt, mixture, logs, gmix, slots, side
        )
        sent, gt, *held = joined(sent, gt, *held)
        near_rest = grid.scatter_z(held)
        held = grid.scatter_plane(kept_qkv, grid.scatter_core(sent))
        grad_rows, back, gains_one = first_back(
            first, tokens, halo, norm_params, full_qkv, gmid, gt
        )
        back, *got = joined(back, *near_rest, *held)
        near_rest, held = got[:4], got[4:]
        near_qkv = grid.scatter_z(held)
        back, *near_qkv = joined(shifted(back, -1), *near_qkv)
        grad_out, grad_up, grad_down, grad_qkv, sums = totals(
            near_rest, near_qkv, gains_one, gains_two
        )
        sums = sums + grid.swap(sums, c=1)
        plane = [grid.swap(sums, y=b, x=a) for a, b in ((1, 0), (0, 1), (1, 1))]
        grad_tokens = after(grad_rows, sums) + back.astype(F32)
        sums = (sums + plane[0]) + (plane[1] + plane[2])
        sums = [sums] + [grid.swap(sums, z=k) for k in (1, 2, 3)]
        *sums, grad_tokens = joined(*sums, grad_tokens)
    else:
        halo = jnp.concatenate([shifted(tokens, k) for k in range(back_steps, 0, -1)])
        full_qkv = beside(whole_of(low_qkv))
        full = tuple(whole_of(a) for a in (low_out, low_up, low_down))
        qkv, kt, vt, xt = project(first, tokens, halo, norm_params, full_qkv)
        mixture, logs = attend(first, low, qkv, vt)
        block_out, gmix, gmid, gains_two, gup, gdown, gout = feed(
            tokens, mixture, cotangent, norm_params, full, full[1].shape[1]
        )
        grad_up, grad_down, grad_out = share_of(gup), share_of(gdown), share_of(gout)
        gt, gqkv = attend_back(first, low, qkv, kt, xt, mixture, logs, gmix)
        grad_qkv = share_of(apart(gqkv))
        grad_rows, back, gains_one = first_back(
            first, tokens, halo, norm_params, full_qkv, gmid, gt
        )
        grad_tokens = grad_rows
        for i, hop in enumerate(range(back_steps, 0, -1)):
            grad_tokens = grad_tokens + shifted(back[i * n : (i + 1) * n], -hop).astype(F32)
        weight_square = (
            jnp.sum(grad_qkv * grad_qkv)
            + jnp.sum(grad_out * grad_out)
            + jnp.sum(grad_up * grad_up)
            + jnp.sum(grad_down * grad_down)
        )
        row = jnp.zeros((4, d), F32).at[0, 0].set(weight_square)
        sums = [lax.psum(jnp.concatenate([gains_one, gains_two, row]), BOTH)]
    step_count = step[0].astype(F32)
    scales = jnp.stack(
        [1.0 - jnp.power(beta_one, step_count), 1.0 - jnp.power(beta_two, step_count)]
    )
    sets, copies, norm_value = adam(
        sums,
        scales,
        (grad_qkv, grad_out, grad_up, grad_down),
        (
            (w_qkv, moment_qkv, square_qkv, average_qkv),
            (w_out.T, moment_out.T, square_out.T, average_out.T),
            (w_up, moment_up, square_up, average_up),
            (w_down.T, moment_down.T, square_down.T, average_down.T),
            (norm_params, moment_norm, square_norm, average_norm),
        ),
    )
    norm_value = norm_value.reshape(())

    def turned(k, value):
        return value.T if k in (1, 3) else value

    return (
        (block_out, grad_tokens, norm_value)
        + tuple(turned(k, s[0]) for k, s in enumerate(sets))
        + tuple(turned(k, s[1]) for k, s in enumerate(sets))
        + tuple(turned(k, s[2]) for k, s in enumerate(sets))
        + tuple(turned(k, c) for k, c in enumerate(copies))
        + tuple(turned(k, s[3]) for k, s in enumerate(sets))
    )


def solution(mesh):
    rows = P(BOTH, None)
    weights = (P(None, "dp", "mp"), P("mp", "dp"), P("dp", "mp"), P("mp", "dp"))
    states = weights + (P(),)
    return jax.shard_map(
        functools.partial(per_device, Grid(mesh.shape["dp"], mesh.shape["mp"])),
        mesh=mesh,
        in_specs=(rows, rows, P("dp"), P("dp"), P()) + states * 4,
        out_specs=(rows, rows, P()) + states * 3 + weights + states,
        check_vma=False,
    )
```

profile of v0, /device:TPU:0, one launch (start us, length us, event | category | flops | bytes accessed | tf_op | source)
XLA Modules:
  0.0 185.8 jit_solution(12599343713259973490)
XLA Ops:
  0.7 2.6 %collective-permute-start.3 = (bf16[1024,512]{1,0:T(8,128)(2,1)}, bf16[1024,512]{1,0:T(8,128)(2,1)S(1)}, u32[]{:S(2)}, u32[]{:S(2)}) collective-permute-start(bf16[1024,512]{1,0:T(8,128)(2,1)} %own_far.1), channel_id=1, source_target_pairs={{0,1},{1,2},{2,3},{4,5},{5,6},{6,7},{8,9},{9,10},{10,11},{12,13},{... | collective-permute-start | bytes 3145736 | tf_op jit(solution)/shard_map/ppermute | solution.py:878
  4.1 2.5 %collective-permute-start = (bf16[64,384]{1,0:T(8,128)(2,1)S(1)}, bf16[64,384]{1,0:T(8,128)(2,1)S(1)}, u32[]{:S(2)}, u32[]{:S(2)}) collective-permute-start(bf16[64,384]{1,0:T(8,128)(2,1)S(1)} %pad_maximum_fusion.3), channel_id=1, source_target_pairs={{0,8},{1,9},{2,10},{3,11},{4,12},{5,13},{6,14},{7,15},{8,0},{9,1},... | collective-permute-start | bytes 147464 | tf_op jit(solution)/shard_map/ppermute | solution.py:651
  6.5 2.6 %collective-permute-start.1 = (bf16[64,384]{1,0:T(8,128)(2,1)S(1)}, bf16[64,384]{1,0:T(8,128)(2,1)S(1)}, u32[]{:S(2)}, u32[]{:S(2)}) collective-permute-start(bf16[64,384]{1,0:T(8,128)(2,1)S(1)} %pad_maximum_fusion.3), channel_id=1, source_target_pairs={{0,16},{1,17},{2,18},{3,19},{4,20},{5,21},{6,22},{7,23},{8,24},{9,... | collective-permute-start | bytes 147464 | tf_op jit(solution)/shard_map/ppermute | solution.py:651
  12.9 2.4 %collective-permute-done.2 = bf16[64,384]{1,0:T(8,128)(2,1)S(1)} collective-permute-done((bf16[64,384]{1,0:T(8,128)(2,1)S(1)}, bf16[64,384]{1,0:T(8,128)(2,1)S(1)}, u32[]{:S(2)}, u32[]{:S(2)}) %collective-permute-start.2) | collective-permute-done | bytes 49184 | tf_op jit(solution)/shard_map/ppermute | solution.py:651
  17.0 2.9 %collective-permute-start.6 = (bf16[64,1152]{1,0:T(8,128)(2,1)S(1)}, bf16[64,1152]{1,0:T(8,128)(2,1)}, u32[]{:S(2)}, u32[]{:S(2)}) collective-permute-start(bf16[64,1152]{1,0:T(8,128)(2,1)S(1)} %pad_maximum_fusion.2), channel_id=1, source_target_pairs={{0,24},{1,25},{2,26},{3,27},{4,28},{5,29},{6,30},{7,31},{8,16},{9,... | collective-permute-start | bytes 442376 | tf_op jit(solution)/shard_map/ppermute | solution.py:651
  22.2 4.6 %collective-permute-start.8 = (bf16[4,64,384]{2,1,0:T(8,128)(2,1)S(1)}, bf16[4,64,384]{2,1,0:T(8,128)(2,1)S(1)}, u32[]{:S(2)}, u32[]{:S(2)}) collective-permute-start(bf16[4,64,384]{2,1,0:T(8,128)(2,1)S(1)} %pad_maximum_fusion.1.refs_4_), channel_id=1, source_target_pairs={{0,2},{1,3},{2,0},{3,1},{4,6},{5,7},{6,4},{7,5},{8,10},{9,11},{10,... | collective-permute-start | bytes 589832 | tf_op jit(solution)/shard_map/ppermute | solution.py:651
  27.9 4.2 %collective-permute-done.8.refs_6_ = bf16[4,64,384]{2,1,0:T(8,128)(2,1)S(1)} collective-permute-done((bf16[4,64,384]{2,1,0:T(8,128)(2,1)S(1)}, bf16[4,64,384]{2,1,0:T(8,128)(2,1)S(1)}, u32[]{:S(2)}, u32[]{:S(2)}) %collective-permute-start.8) | collective-permute-done | bytes 196640 | tf_op jit(solution)/shard_map/ppermute | solution.py:651
  32.1 2.5 %collective-permute-done.9.refs_7_ = bf16[4,64,384]{2,1,0:T(8,128)(2,1)S(1)} collective-permute-done((bf16[4,64,384]{2,1,0:T(8,128)(2,1)S(1)}, bf16[4,64,384]{2,1,0:T(8,128)(2,1)S(1)}, u32[]{:S(2)}, u32[]{:S(2)}) %collective-permute-start.9) | collective-permute-done | bytes 196640 | tf_op jit(solution)/shard_map/ppermute | solution.py:651
  40.5 5.7 %shard_map.439 = (bf16[2048,1536]{1,0:T(8,128)(2,1)S(1)}, bf16[512,2048]{1,0:T(8,128)(2,1)S(1)}, bf16[512,2048]{1,0:T(8,128)(2,1)S(1)}, bf16[512,2048]{1,0:T(8,128)(2,1)S(1)}, bf16[512,1536]{1,0:T(8,128)(2,1)S(1)}) custom-call(s32[4]{0:T(128)S(1)} %and_select_fusion.first_ref, s32[32]{0:T(128)S(1)} %xor_add_fusion.1.refs_0_, f32[4,512]{1,0:T(4,128)S(1)} %copy-done.21, ...), custom_call_target="tpu_custom_call" | custom-call | flops 3221225472 | bytes 16252928 | tf_op jit(solution)/shard_map/pallas_call | solution.py:50
  46.2 12.8 %shard_map.440 = (bf16[1024,512]{1,0:T(8,128)(2,1)S(1)}, f32[8,1024]{1,0:T(8,128)S(1)}) custom-call(s32[4]{0:T(128)S(1)} %and_select_fusion.first_ref, s32[1,1024]{1,0:T(1,128)S(1)} %bitcast.58, bf16[2048,1536]{1,0:T(8,128)(2,1)S(1)} %get-tuple-element.129.qkv_ref.refs_3_, bf16[512,2048]{1,0:T(8,128)(2,1)S(1)} %get-tuple-element.130.vt_ref), custom_call_target="tpu_custom_call" | custom-call | flops 8589934592 | bytes 10485760 | tf_op jit(solution)/shard_map/pallas_call | solution.py:50
  59.1 6.0 %collective-permute-done.16.refs_10_ = bf16[4,64,1152]{2,1,0:T(8,128)(2,1)} collective-permute-done((bf16[4,64,1152]{2,1,0:T(8,128)(2,1)S(1)}, bf16[4,64,1152]{2,1,0:T(8,128)(2,1)}, u32[]{:S(2)}, u32[]{:S(2)}) %collective-permute-start.16) | collective-permute-done | bytes 589856 | tf_op jit(solution)/shard_map/ppermute | solution.py:651
  70.0 21.6 %shard_map.441 = (bf16[1024,512]{1,0:T(8,128)(2,1)}, bf16[1024,512]{1,0:T(8,128)(2,1)S(1)}, f32[1024,512]{1,0:T(8,128)S(1)}, f32[2,512]{1,0:T(2,128)S(1)}, bf16[...) custom-call(s32[32]{0:T(128)S(1)} %xor_add_fusion.1.refs_0_, ...), custom_call_target="tpu_custom_call" | custom-call | flops 14495514624 | bytes 14680064 | tf_op jit(solution)/shard_map/pallas_call | solution.py:50
  91.9 3.5 %shard_map.442 = bf16[16,64,1152]{2,1,0:T(8,128)(2,1)S(1)} custom-call(s32[32]{0:T(128)S(1)} %xor_add_fusion.refs_1_.slots_ref.refs_0_, s32[2]{0:T(128)S(1)} %pad_add_fusion.refs_2_.side_ref.refs_1_, bf16[1024,512]{1,0:T(8,128)(2,1)S(1)} %get-tuple-element.133.refs_3_.refs_0_.refs_6_, bf16[1024,1024]{1,0:T(8,128)(2,1)S(1)} %get-tuple-element.146.refs_1_, ...), custom_call_target="tpu_custom_call" | custom-call | flops 2415919104 | bytes 8388608 | tf_op jit(solution)/shard_map/pallas_call | solution.py:50
  100.6 22.8 %shard_map.443 = (bf16[1536,2048]{1,0:T(8,128)(2,1)S(1)}, bf16[16,64,384]{2,1,0:T(8,128)(2,1)S(1)}, bf16[16,64,384]{2,1,0:T(8,128)(2,1)S(1)}) custom-call(s32[4]{0:T(128)S(1)} %and_select_fusion.first_ref, s32[32]{0:T(128)S(1)} %xor_add_fusion.refs_1_.slots_ref.refs_0_, s32[2]{0:T(128)S(1)} %pad_add_fusion.refs_2_.side_ref.refs_1_, s32[1,1024]{1,0:T(1,128)S(1)} %bitcast.59, ...), custom_call_target="tpu_custom_call" | custom-call | flops 21474836480 | bytes 18874368 | tf_op jit(solution)/shard_map/pallas_call | solution.py:50
  123.4 2.9 %collective-permute-done.24 = bf16[4,64,1152]{2,1,0:T(8,128)(2,1)S(1)} collective-permute-done((bf16[4,64,1152]{2,1,0:T(8,128)(2,1)S(1)}, bf16[4,64,1152]{2,1,0:T(8,128)(2,1)S(1)}, u32[]{:S(2)}, u32[]{:S(2)}) %collective-permute-start.24) | collective-permute-done | bytes 589856 | tf_op jit(solution)/shard_map/ppermute | solution.py:651
  127.1 3.7 %collective-permute-start.26 = (bf16[64,1152]{1,0:T(8,128)(2,1)S(1)}, bf16[64,1152]{1,0:T(8,128)(2,1)S(1)}, u32[]{:S(2)}, u32[]{:S(2)}) collective-permute-start(bf16[64,1152]{1,0:T(8,128)(2,1)S(1)} %get-tuple-element.222), channel_id=1, source_target_pairs={{0,16},{1,17},{2,18},{3,19},{4,20},{5,21},{6,22},{7,23},{8,24},{9,... | collective-permute-start | bytes 442376 | tf_op jit(solution)/shard_map/ppermute | solution.py:651
  132.8 8.2 %collective-permute-start.30 = (bf16[4,64,384]{2,1,0:T(8,128)(2,1)S(1)}, bf16[4,64,384]{2,1,0:T(8,128)(2,1)S(1)}, u32[]{:S(2)}, u32[]{:S(2)}) collective-permute-start(bf16[4,64,384]{2,1,0:T(8,128)(2,1)S(1)} %get-tuple-element.226), channel_id=1, source_target_pairs={{0,2},{1,3},{2,0},{3,1},{4,6},{5,7},{6,4},{7,5},{8,10},{9,11},{10,... | collective-permute-start | bytes 589832 | tf_op jit(solution)/shard_map/ppermute | solution.py:651
  141.0 3.0 %collective-permute-start.31 = (bf16[4,64,384]{2,1,0:T(8,128)(2,1)S(1)}, bf16[4,64,384]{2,1,0:T(8,128)(2,1)S(1)}, u32[]{:S(2)}, u32[]{:S(2)}) collective-permute-start(bf16[4,64,384]{2,1,0:T(8,128)(2,1)S(1)} %get-tuple-element.225), channel_id=1, source_target_pairs={{0,6},{1,7},{2,4},{3,5},{4,2},{5,3},{6,0},{7,1},{8,14},{9,15},{10,... | collective-permute-start | bytes 589832 | tf_op jit(solution)/shard_map/ppermute | solution.py:651
  144.0 4.2 %shard_map.444 = (f32[1024,512]{1,0:T(8,128)S(1)}, bf16[1024,512]{1,0:T(8,128)(2,1)S(1)}, f32[2,512]{1,0:T(2,128)S(1)}) custom-call(s32[4]{0:T(128)S(1)} %and_select_fusion.first_ref, f32[4,512]{1,0:T(4,128)S(1)} %copy-done.21, bf16[512,1536]{1,0:T(8,128)(2,1)S(1)} %get-tuple-element.139.w_ref, f32[1024,512]{1,0:T(8,128)S(1)} %get-tuple-element.140.gmid_ref, ...), custom_call_target="tpu_custom_call" | custom-call | flops 3221225472 | bytes 14680064 | tf_op jit(solution)/shard_map/pallas_call | solution.py:50
  156.4 2.7 %collective-permute-done.35.refs_7_ = bf16[64,384]{1,0:T(8,128)(2,1)S(1)} collective-permute-done((bf16[64,384]{1,0:T(8,128)(2,1)S(1)}, bf16[64,384]{1,0:T(8,128)(2,1)S(1)}, u32[]{:S(2)}, u32[]{:S(2)}) %collective-permute-start.35) | collective-permute-done | bytes 49184 | tf_op jit(solution)/shard_map/ppermute | solution.py:651
  159.3 6.6 %collective-permute-start.36 = (f32[8,512]{1,0:T(8,128)S(1)}, f32[8,512]{1,0:T(8,128)S(1)}, u32[]{:S(2)}, u32[]{:S(2)}) collective-permute-start(f32[8,512]{1,0:T(8,128)S(1)} %get-tuple-element.179), channel_id=1, source_target_pairs={{0,1},{1,0},{2,3},{3,2},{4,5},{5,4},{6,7},{7,6},{8,9},{9,8},{10,11... | collective-permute-start | bytes 49160 | tf_op jit(solution)/shard_map/ppermute | solution.py:651
  170.5 2.6 %collective-permute-done.39 = f32[8,512]{1,0:T(8,128)S(1)} collective-permute-done((f32[8,512]{1,0:T(8,128)S(1)}, f32[8,512]{1,0:T(8,128)S(1)}, u32[]{:S(2)}, u32[]{:S(2)}) %collective-permute-start.39) | collective-permute-done | bytes 16416 | tf_op jit(solution)/shard_map/ppermute | solution.py:651
  175.4 2.3 %collective-permute-start.42 = (f32[8,512]{1,0:T(8,128)S(1)}, f32[8,512]{1,0:T(8,128)S(1)}, u32[]{:S(2)}, u32[]{:S(2)}) collective-permute-start(f32[8,512]{1,0:T(8,128)S(1)} %add_add_fusion.refs_0_), channel_id=1, source_target_pairs={{0,24},{1,25},{2,26},{3,27},{4,28},{5,29},{6,30},{7,31},{8,16},{9,... | collective-permute-start | bytes 49160 | tf_op jit(solution)/shard_map/ppermute | solution.py:651
  181.1 4.5 %shard_map.446 = (f32[3,64,128]{2,1,0:T(8,128)}, f32[3,64,128]{2,1,0:T(8,128)}, f32[3,64,128]{2,1,0:T(8,128)}, f32[3,64,128]{2,1,0:T(8,128)}, f32[64,128]{1,0:T(...) custom-call(f32[2]{0:T(128)S(1)} %pad_maximum_fusion.4.scale_ref, ...), custom_call_target="tpu_custom_call" | custom-call | flops 3010560 | bytes 3813376 | tf_op jit(solution)/shard_map/pallas_call | solution.py:50
  (152 shorter events, 46.2 us)
Async XLA Ops:
  0.7 14.7 %collective-permute-start.3 = (bf16[1024,512]{1,0:T(8,128)(2,1)}, bf16[1024,512]{1,0:T(8,128)(2,1)S(1)}, u32[]{:S(2)}, u32[]{:S(2)}) collective-permute-start(bf16[1024,512]{1,0:T(8,128)(2,1)} %own_far.1), channel_id=1, source_target_pairs={{0,1},{1,2},{2,3},{4,5},{5,6},{6,7},{8,9},{9,10},{10,11},{12,13},{... | collective-permute-start | bytes 3145736 | tf_op jit(solution)/shard_map/ppermute | solution.py:878
  4.1 7.7 %collective-permute-start = (bf16[64,384]{1,0:T(8,128)(2,1)S(1)}, bf16[64,384]{1,0:T(8,128)(2,1)S(1)}, u32[]{:S(2)}, u32[]{:S(2)}) collective-permute-start(bf16[64,384]{1,0:T(8,128)(2,1)S(1)} %pad_maximum_fusion.3), channel_id=1, source_target_pairs={{0,8},{1,9},{2,10},{3,11},{4,12},{5,13},{6,14},{7,15},{8,0},{9,1},... | collective-permute-start | bytes 147464 | tf_op jit(solution)/shard_map/ppermute | solution.py:651
  6.5 6.4 %collective-permute-start.1 = (bf16[64,384]{1,0:T(8,128)(2,1)S(1)}, bf16[64,384]{1,0:T(8,128)(2,1)S(1)}, u32[]{:S(2)}, u32[]{:S(2)}) collective-permute-start(bf16[64,384]{1,0:T(8,128)(2,1)S(1)} %pad_maximum_fusion.3), channel_id=1, source_target_pairs={{0,16},{1,17},{2,18},{3,19},{4,20},{5,21},{6,22},{7,23},{8,24},{9,... | collective-permute-start | bytes 147464 | tf_op jit(solution)/shard_map/ppermute | solution.py:651
  9.1 6.2 %collective-permute-start.2 = (bf16[64,384]{1,0:T(8,128)(2,1)S(1)}, bf16[64,384]{1,0:T(8,128)(2,1)S(1)}, u32[]{:S(2)}, u32[]{:S(2)}) collective-permute-start(bf16[64,384]{1,0:T(8,128)(2,1)S(1)} %pad_maximum_fusion.3), channel_id=1, source_target_pairs={{0,24},{1,25},{2,26},{3,27},{4,28},{5,29},{6,30},{7,31},{8,16},{9,... | collective-permute-start | bytes 147464 | tf_op jit(solution)/shard_map/ppermute | solution.py:651
  15.4 11.4 %collective-permute-start.4 = (bf16[64,1152]{1,0:T(8,128)(2,1)S(1)}, bf16[64,1152]{1,0:T(8,128)(2,1)S(1)}, u32[]{:S(2)}, u32[]{:S(2)}) collective-permute-start(bf16[64,1152]{1,0:T(8,128)(2,1)S(1)} %pad_maximum_fusion.2), channel_id=1, source_target_pairs={{0,8},{1,9},{2,10},{3,11},{4,12},{5,13},{6,14},{7,15},{8,0},{9,1},... | collective-permute-start | bytes 442376 | tf_op jit(solution)/shard_map/ppermute | solution.py:651
  15.5 11.4 %collective-permute-start.5 = (bf16[64,1152]{1,0:T(8,128)(2,1)S(1)}, bf16[64,1152]{1,0:T(8,128)(2,1)S(1)}, u32[]{:S(2)}, u32[]{:S(2)}) collective-permute-start(bf16[64,1152]{1,0:T(8,128)(2,1)S(1)} %pad_maximum_fusion.2), channel_id=1, source_target_pairs={{0,16},{1,17},{2,18},{3,19},{4,20},{5,21},{6,22},{7,23},{8,24},{9,... | collective-permute-start | bytes 442376 | tf_op jit(solution)/shard_map/ppermute | solution.py:651
  17.0 9.9 %collective-permute-start.6 = (bf16[64,1152]{1,0:T(8,128)(2,1)S(1)}, bf16[64,1152]{1,0:T(8,128)(2,1)}, u32[]{:S(2)}, u32[]{:S(2)}) collective-permute-start(bf16[64,1152]{1,0:T(8,128)(2,1)S(1)} %pad_maximum_fusion.2), channel_id=1, source_target_pairs={{0,24},{1,25},{2,26},{3,27},{4,28},{5,29},{6,30},{7,31},{8,16},{9,... | collective-permute-start | bytes 442376 | tf_op jit(solution)/shard_map/ppermute | solution.py:651
  20.7 7.3 %collective-permute-start.7 = (bf16[4,64,384]{2,1,0:T(8,128)(2,1)S(1)}, bf16[4,64,384]{2,1,0:T(8,128)(2,1)S(1)}, u32[]{:S(2)}, u32[]{:S(2)}) collective-permute-start(bf16[4,64,384]{2,1,0:T(8,128)(2,1)S(1)} %pad_maximum_fusion.1.refs_4_), channel_id=1, source_target_pairs={{0,4},{1,5},{2,6},{3,7},{4,0},{5,1},{6,2},{7,3},{8,12},{9,13},{10,... | collective-permute-start | bytes 589832 | tf_op jit(solution)/shard_map/ppermute | solution.py:651
  22.2 9.9 %collective-permute-start.8 = (bf16[4,64,384]{2,1,0:T(8,128)(2,1)S(1)}, bf16[4,64,384]{2,1,0:T(8,128)(2,1)S(1)}, u32[]{:S(2)}, u32[]{:S(2)}) collective-permute-start(bf16[4,64,384]{2,1,0:T(8,128)(2,1)S(1)} %pad_maximum_fusion.1.refs_4_), channel_id=1, source_target_pairs={{0,2},{1,3},{2,0},{3,1},{4,6},{5,7},{6,4},{7,5},{8,10},{9,11},{10,... | collective-permute-start | bytes 589832 | tf_op jit(solution)/shard_map/ppermute | solution.py:651
  26.9 7.8 %collective-permute-start.9 = (bf16[4,64,384]{2,1,0:T(8,128)(2,1)S(1)}, bf16[4,64,384]{2,1,0:T(8,128)(2,1)S(1)}, u32[]{:S(2)}, u32[]{:S(2)}) collective-permute-start(bf16[4,64,384]{2,1,0:T(8,128)(2,1)S(1)} %pad_maximum_fusion.1.refs_4_), channel_id=1, source_target_pairs={{0,6},{1,7},{2,4},{3,5},{4,2},{5,3},{6,0},{7,1},{8,14},{9,15},{10,... | collective-permute-start | bytes 589832 | tf_op jit(solution)/shard_map/ppermute | solution.py:651
  35.7 23.4 %collective-permute-start.14 = (bf16[4,64,1152]{2,1,0:T(8,128)(2,1)S(1)}, bf16[4,64,1152]{2,1,0:T(8,128)(2,1)}, u32[]{:S(2)}, u32[]{:S(2)}) collective-permute-start(bf16[4,64,1152]{2,1,0:T(8,128)(2,1)S(1)} %pad_maximum_fusion.refs_7_), channel_id=1, source_target_pairs={{0,4},{1,5},{2,6},{3,7},{4,0},{5,1},{6,2},{7,3},{8,12},{9,13},{10,... | collective-permute-start | bytes 1769480 | tf_op jit(solution)/shard_map/ppermute | solution.py:651
  37.3 21.9 %collective-permute-start.15 = (bf16[4,64,1152]{2,1,0:T(8,128)(2,1)S(1)}, bf16[4,64,1152]{2,1,0:T(8,128)(2,1)}, u32[]{:S(2)}, u32[]{:S(2)}) collective-permute-start(bf16[4,64,1152]{2,1,0:T(8,128)(2,1)S(1)} %pad_maximum_fusion.refs_7_), channel_id=1, source_target_pairs={{0,2},{1,3},{2,0},{3,1},{4,6},{5,7},{6,4},{7,5},{8,10},{9,11},{10,... | collective-permute-start | bytes 1769480 | tf_op jit(solution)/shard_map/ppermute | solution.py:651
  37.4 27.8 %collective-permute-start.16 = (bf16[4,64,1152]{2,1,0:T(8,128)(2,1)S(1)}, bf16[4,64,1152]{2,1,0:T(8,128)(2,1)}, u32[]{:S(2)}, u32[]{:S(2)}) collective-permute-start(bf16[4,64,1152]{2,1,0:T(8,128)(2,1)S(1)} %pad_maximum_fusion.refs_7_), channel_id=1, source_target_pairs={{0,6},{1,7},{2,4},{3,5},{4,2},{5,3},{6,0},{7,1},{8,14},{9,15},{10,... | collective-permute-start | bytes 1769480 | tf_op jit(solution)/shard_map/ppermute | solution.py:651
  97.0 26.4 %collective-permute-start.22 = (bf16[4,64,1152]{2,1,0:T(8,128)(2,1)S(1)}, bf16[4,64,1152]{2,1,0:T(8,128)(2,1)S(1)}, u32[]{:S(2)}, u32[]{:S(2)}) collective-permute-start(bf16[4,64,1152]{2,1,0:T(8,128)(2,1)S(1)} %get-tuple-element.219), channel_id=1, source_target_pairs={{0,4},{1,5},{2,6},{3,7},{4,0},{5,1},{6,2},{7,3},{8,12},{9,13},{10,... | collective-permute-start | bytes 1769480 | tf_op jit(solution)/shard_map/ppermute | solution.py:651
  98.3 25.1 %collective-permute-start.23 = (bf16[4,64,1152]{2,1,0:T(8,128)(2,1)S(1)}, bf16[4,64,1152]{2,1,0:T(8,128)(2,1)S(1)}, u32[]{:S(2)}, u32[]{:S(2)}) collective-permute-start(bf16[4,64,1152]{2,1,0:T(8,128)(2,1)S(1)} %get-tuple-element.218), channel_id=1, source_target_pairs={{0,2},{1,3},{2,0},{3,1},{4,6},{5,7},{6,4},{7,5},{8,10},{9,11},{10,... | collective-permute-start | bytes 1769480 | tf_op jit(solution)/shard_map/ppermute | solution.py:651
  100.3 26.0 %collective-permute-start.24 = (bf16[4,64,1152]{2,1,0:T(8,128)(2,1)S(1)}, bf16[4,64,1152]{2,1,0:T(8,128)(2,1)S(1)}, u32[]{:S(2)}, u32[]{:S(2)}) collective-permute-start(bf16[4,64,1152]{2,1,0:T(8,128)(2,1)S(1)} %get-tuple-element.217), channel_id=1, source_target_pairs={{0,6},{1,7},{2,4},{3,5},{4,2},{5,3},{6,0},{7,1},{8,14},{9,15},{10,... | collective-permute-start | bytes 1769480 | tf_op jit(solution)/shard_map/ppermute | solution.py:651
  126.6 14.4 %collective-permute-start.25 = (bf16[64,1152]{1,0:T(8,128)(2,1)S(1)}, bf16[64,1152]{1,0:T(8,128)(2,1)S(1)}, u32[]{:S(2)}, u32[]{:S(2)}) collective-permute-start(bf16[64,1152]{1,0:T(8,128)(2,1)S(1)} %get-tuple-element.223), channel_id=1, source_target_pairs={{0,8},{1,9},{2,10},{3,11},{4,12},{5,13},{6,14},{7,15},{8,0},{9,1},... | collective-permute-start | bytes 442376 | tf_op jit(solution)/shard_map/ppermute | solution.py:651
  127.1 21.1 %collective-permute-start.26 = (bf16[64,1152]{1,0:T(8,128)(2,1)S(1)}, bf16[64,1152]{1,0:T(8,128)(2,1)S(1)}, u32[]{:S(2)}, u32[]{:S(2)}) collective-permute-start(bf16[64,1152]{1,0:T(8,128)(2,1)S(1)} %get-tuple-element.222), channel_id=1, source_target_pairs={{0,16},{1,17},{2,18},{3,19},{4,20},{5,21},{6,22},{7,23},{8,24},{9,... | collective-permute-start | bytes 442376 | tf_op jit(solution)/shard_map/ppermute | solution.py:651
  130.8 17.4 %collective-permute-start.27 = (bf16[64,1152]{1,0:T(8,128)(2,1)S(1)}, bf16[64,1152]{1,0:T(8,128)(2,1)S(1)}, u32[]{:S(2)}, u32[]{:S(2)}) collective-permute-start(bf16[64,1152]{1,0:T(8,128)(2,1)S(1)} %get-tuple-element.221), channel_id=1, source_target_pairs={{0,24},{1,25},{2,26},{3,27},{4,28},{5,29},{6,30},{7,31},{8,16},{9,... | collective-permute-start | bytes 442376 | tf_op jit(solution)/shard_map/ppermute | solution.py:651
  131.2 17.0 %collective-permute-start.29 = (bf16[4,64,384]{2,1,0:T(8,128)(2,1)S(1)}, bf16[4,64,384]{2,1,0:T(8,128)(2,1)S(1)}, u32[]{:S(2)}, u32[]{:S(2)}) collective-permute-start(bf16[4,64,384]{2,1,0:T(8,128)(2,1)S(1)} %get-tuple-element.227), channel_id=1, source_target_pairs={{0,4},{1,5},{2,6},{3,7},{4,0},{5,1},{6,2},{7,3},{8,12},{9,13},{10,... | collective-permute-start | bytes 589832 | tf_op jit(solution)/shard_map/ppermute | solution.py:651
  132.8 15.5 %collective-permute-start.30 = (bf16[4,64,384]{2,1,0:T(8,128)(2,1)S(1)}, bf16[4,64,384]{2,1,0:T(8,128)(2,1)S(1)}, u32[]{:S(2)}, u32[]{:S(2)}) collective-permute-start(bf16[4,64,384]{2,1,0:T(8,128)(2,1)S(1)} %get-tuple-element.226), channel_id=1, source_target_pairs={{0,2},{1,3},{2,0},{3,1},{4,6},{5,7},{6,4},{7,5},{8,10},{9,11},{10,... | collective-permute-start | bytes 589832 | tf_op jit(solution)/shard_map/ppermute | solution.py:651
  141.0 8.4 %collective-permute-start.31 = (bf16[4,64,384]{2,1,0:T(8,128)(2,1)S(1)}, bf16[4,64,384]{2,1,0:T(8,128)(2,1)S(1)}, u32[]{:S(2)}, u32[]{:S(2)}) collective-permute-start(bf16[4,64,384]{2,1,0:T(8,128)(2,1)S(1)} %get-tuple-element.225), channel_id=1, source_target_pairs={{0,6},{1,7},{2,4},{3,5},{4,2},{5,3},{6,0},{7,1},{8,14},{9,15},{10,... | collective-permute-start | bytes 589832 | tf_op jit(solution)/shard_map/ppermute | solution.py:651
  149.4 9.7 %collective-permute-start.32 = (bf16[1024,512]{1,0:T(8,128)(2,1)S(1)}, bf16[1024,512]{1,0:T(8,128)(2,1)S(1)}, u32[]{:S(2)}, u32[]{:S(2)}) collective-permute-start(bf16[1024,512]{1,0:T(8,128)(2,1)S(1)} %get-tuple-element.168), channel_id=1, source_target_pairs={{1,0},{2,1},{3,2},{5,4},{6,5},{7,6},{9,8},{10,9},{11,10},{13,12},{... | collective-permute-start | bytes 3145736 | tf_op jit(solution)/shard_map/ppermute | solution.py:878
  159.3 7.4 %collective-permute-start.36 = (f32[8,512]{1,0:T(8,128)S(1)}, f32[8,512]{1,0:T(8,128)S(1)}, u32[]{:S(2)}, u32[]{:S(2)}) collective-permute-start(f32[8,512]{1,0:T(8,128)S(1)} %get-tuple-element.179), channel_id=1, source_target_pairs={{0,1},{1,0},{2,3},{3,2},{4,5},{5,4},{6,7},{7,6},{8,9},{9,8},{10,11... | collective-permute-start | bytes 49160 | tf_op jit(solution)/shard_map/ppermute | solution.py:651
  (49 other events, 416.1 us)
where the time goes:
time: 185 us; the launch traced here: 186 us
  Pallas kernels  75.3 us (41%)
  starting transfers between devices  65 us (35%)
  waiting for transfers between devices  33.5 us (18%)
  other arithmetic  7.49 us (4%)
  local copies, waits for them, and re-layouts  2.27 us (1%)
  between operations  2.24 us (1%)
    pallas_call x8, Pallas kernels, call(): pl.pallas_call(body, out_shape=outs, in_specs=[pl.BlockSpec(memory_space=...  75.3 us
    ppermute x41, starting transfers between devices, swap(): lax.ppermute(value, BOTH, [(i, i ^ bits) for i in range(self.dp * self.mp)])  61.2 us
    ppermute x41, waiting for transfers between devices, swap(): lax.ppermute(value, BOTH, [(i, i ^ bits) for i in range(self.dp * self.mp)])  33.5 us
    ppermute x2, starting transfers between devices, shifted(): return lax.ppermute(value, 'mp', pairs)  3.84 us
  transfers between devices with their start and end apart: 43, of which 21 were waited for; matrix products, arithmetic and copies ran while one was open for 4% of the time, Pallas kernels for 26%

commit v1 on v0

--- a/solution.py
+++ b/solution.py
@@ -796,10 +796,29 @@
     )
 
 
+def load_body(*refs):
+    count = len(refs) // 2
+    copies = fetch(tuple(zip(refs[:count], refs[count:-1])), refs[-1])
+    for copy in copies:
+        copy.wait()
+
+
+def load(values):
+    return call(
+        load_body,
+        tuple(shape(v.shape, v.dtype) for v in values),
+        (),
+        (),
+        tuple(in_hbm(v) for v in values),
+        (pltpu.SemaphoreType.DMA((len(values),)),),
+        moved=8 * sum(v.size for v in values),
+        room=16,
+    )
+
+
 def adam_body(parts, scale_ref, *refs):
     sums, grads, refs = refs[:parts], refs[parts : parts + 4], refs[parts + 4 :]
-    far, outs, norm_ref, held, sems = refs[:20], refs[20:44], refs[44], refs[45:65], refs[65]
-    copies = fetch(tuple(zip(far, held)), sems)
+    held, outs, norm_ref = refs[:20], refs[20:44], refs[44]
     total = sums[0][...]
     if parts == 4:
         total = (total + sums[1][...]) + (sums[2][...] + sums[3][...])
@@ -809,8 +828,6 @@
     norm_ref[0, 0] = jnp.sum(norm)
     factor = jnp.minimum(1.0, clip_limit / (norm + 1e-06))
     fixed_one, fixed_two = scale_ref[0], scale_ref[1]
-    for copy in copies:
-        copy.wait()
     for k, (rate, decay) in enumerate(RATES):
         weight, moment, square, average = (ref[...] for ref in held[4 * k : 4 * k + 4])
         grad = grads[k][...] if k < 4 else gains
@@ -830,9 +847,7 @@
         functools.partial(adam_body, len(sums)),
         outs,
         (scales,),
-        tuple(sums) + tuple(grads),
-        sum((tuple(s) for s in sets), ()),
-        tuple(VMEM(a.shape, F32) for s in sets for a in s) + (pltpu.SemaphoreType.DMA((20,)),),
+        tuple(sums) + tuple(grads) + sum((tuple(s) for s in sets), ()),
         flops=30 * sum(s[0].size for s in sets),
         moved=38 * sum(s[0].size for s in sets),
         room=16,
@@ -922,15 +937,16 @@
         back, *got = joined(back, *near_rest, *held)
         near_rest, held = got[:4], got[4:]
         near_qkv = grid.scatter_z(held)
-        back, *near_qkv = joined(shifted(back, -1), *near_qkv)
+        near_qkv = joined(*near_qkv)
+        back = shifted(after(back, near_qkv[1]), -1)
         grad_out, grad_up, grad_down, grad_qkv, sums = totals(
             near_rest, near_qkv, gains_one, gains_two
         )
         sums = sums + grid.swap(sums, c=1)
-        plane = [grid.swap(sums, y=b, x=a) for a, b in ((1, 0), (0, 1), (1, 1))]
-        grad_tokens = after(grad_rows, sums) + back.astype(F32)
-        sums = (sums + plane[0]) + (plane[1] + plane[2])
-        sums = [sums] + [grid.swap(sums, z=k) for k in (1, 2, 3)]
+        line = [grid.swap(sums, z=k) for k in (1, 2, 3)]
+        sums = (sums + line[0]) + (line[1] + line[2])
+        grad_tokens = grad_rows + back.astype(F32)
+        sums = [sums] + [grid.swap(sums, y=b, x=a) for a, b in ((1, 0), (0, 1), (1, 1))]
         *sums, grad_tokens = joined(*sums, grad_tokens)
     else:
         halo = jnp.concatenate([shifted(tokens, k) for k in range(back_steps, 0, -1)])
@@ -962,17 +978,18 @@
     scales = jnp.stack(
         [1.0 - jnp.power(beta_one, step_count), 1.0 - jnp.power(beta_two, step_count)]
     )
+    states = (
+        (w_qkv, moment_qkv, square_qkv, average_qkv),
+        (w_out.T, moment_out.T, square_out.T, average_out.T),
+        (w_up, moment_up, square_up, average_up),
+        (w_down.T, moment_down.T, square_down.T, average_down.T),
+        (norm_params, moment_norm, square_norm, average_norm),
+    )
+    if grid.fast:
+        flat = load(sum(states, ()))
+        states = tuple(tuple(flat[4 * k : 4 * k + 4]) for k in range(5))
     sets, copies, norm_value = adam(
-        sums,
-        scales,
-        (grad_qkv, grad_out, grad_up, grad_down),
-        (
-            (w_qkv, moment_qkv, square_qkv, average_qkv),
-            (w_out.T, moment_out.T, square_out.T, average_out.T),
-            (w_up, moment_up, square_up, average_up),
-            (w_down.T, moment_down.T, square_down.T, average_down.T),
-            (norm_params, moment_norm, square_norm, average_norm),
-        ),
+        sums, scales, (grad_qkv, grad_out, grad_up, grad_down), states
     )
     norm_value = norm_value.reshape(())
 

time: 185 us -> 178 us (0.962); the launches traced: 186 us -> 177 us
  starting transfers between devices: 65 us -> 52.6 us
  waiting for transfers between devices: 33.5 us -> 38.2 us
    ppermute x41, starting transfers between devices: 61.2 us -> 48.7 us  [swap(): lax.ppermute(value, BOTH, [(i, i ^ bits) for i in range(self.dp * self.mp)])]
    ppermute x41, waiting for transfers between devices: 33.5 us -> 38.2 us  [swap(): lax.ppermute(value, BOTH, [(i, i ^ bits) for i in range(self.dp * self.mp)])]
    pallas_call x8 -> x9, Pallas kernels: 75.3 us -> 74.4 us  [call(): pl.pallas_call(body, out_shape=outs, in_specs=[pl.BlockSpec(memory_space=...]
  transfers between devices with their start and end apart: 43 -> 43, of which waited for: 21 -> 22; matrix products, arithmetic and copies ran while one was open for 4% -> 4% of each run, Pallas kernels for 26% -> 29%
where the time goes in v1:
time: 178 us; the launch traced here: 177 us
  Pallas kernels  74.4 us (42%)
  starting transfers between devices  52.6 us (30%)
  waiting for transfers between devices  38.2 us (21%)
  other arithmetic  7.48 us (4%)
  local copies, waits for them, and re-layouts  2.16 us (1%)
  between operations  1.96 us (1%)
    pallas_call x9, Pallas kernels, call(): pl.pallas_call(body, out_shape=outs, in_specs=[pl.BlockSpec(memory_space=...  74.4 us
    ppermute x41, starting transfers between devices, swap(): lax.ppermute(value, BOTH, [(i, i ^ bits) for i in range(self.dp * self.mp)])  48.7 us
    ppermute x41, waiting for transfers between devices, swap(): lax.ppermute(value, BOTH, [(i, i ^ bits) for i in range(self.dp * self.mp)])  38.2 us
    ppermute x2, starting transfers between devices, shifted(): return lax.ppermute(value, 'mp', pairs)  3.84 us
  transfers between devices with their start and end apart: 43, of which 22 were waited for; matrix products, arithmetic and copies ran while one was open for 4% of the time, Pallas kernels for 29%

profile of v1, /device:TPU:0, one launch (start us, length us, event | category | flops | bytes accessed | tf_op | source)
XLA Modules:
  0.0 176.8 jit_solution(13563659941543395448)
XLA Ops:
  0.7 2.6 %collective-permute-start.3 = (bf16[1024,512]{1,0:T(8,128)(2,1)}, bf16[1024,512]{1,0:T(8,128)(2,1)S(1)}, u32[]{:S(2)}, u32[]{:S(2)}) collective-permute-start(bf16[1024,512]{1,0:T(8,128)(2,1)} %own_far.1), channel_id=1, source_target_pairs={{0,1},{1,2},{2,3},{4,5},{5,6},{6,7},{8,9},{9,10},{10,11},{12,13},{... | collective-permute-start | bytes 3145736 | tf_op jit(solution)/shard_map/ppermute | solution.py:893
  4.1 2.5 %collective-permute-start = (bf16[64,384]{1,0:T(8,128)(2,1)S(1)}, bf16[64,384]{1,0:T(8,128)(2,1)S(1)}, u32[]{:S(2)}, u32[]{:S(2)}) collective-permute-start(bf16[64,384]{1,0:T(8,128)(2,1)S(1)} %pad_maximum_fusion.3), channel_id=1, source_target_pairs={{0,8},{1,9},{2,10},{3,11},{4,12},{5,13},{6,14},{7,15},{8,0},{9,1},... | collective-permute-start | bytes 147464 | tf_op jit(solution)/shard_map/ppermute | solution.py:651
  6.5 2.6 %collective-permute-start.1 = (bf16[64,384]{1,0:T(8,128)(2,1)S(1)}, bf16[64,384]{1,0:T(8,128)(2,1)S(1)}, u32[]{:S(2)}, u32[]{:S(2)}) collective-permute-start(bf16[64,384]{1,0:T(8,128)(2,1)S(1)} %pad_maximum_fusion.3), channel_id=1, source_target_pairs={{0,16},{1,17},{2,18},{3,19},{4,20},{5,21},{6,22},{7,23},{8,24},{9,... | collective-permute-start | bytes 147464 | tf_op jit(solution)/shard_map/ppermute | solution.py:651
  12.9 2.4 %collective-permute-done.2 = bf16[64,384]{1,0:T(8,128)(2,1)S(1)} collective-permute-done((bf16[64,384]{1,0:T(8,128)(2,1)S(1)}, bf16[64,384]{1,0:T(8,128)(2,1)S(1)}, u32[]{:S(2)}, u32[]{:S(2)}) %collective-permute-start.2) | collective-permute-done | bytes 49184 | tf_op jit(solution)/shard_map/ppermute | solution.py:651
  17.0 2.9 %collective-permute-start.6 = (bf16[64,1152]{1,0:T(8,128)(2,1)S(1)}, bf16[64,1152]{1,0:T(8,128)(2,1)}, u32[]{:S(2)}, u32[]{:S(2)}) collective-permute-start(bf16[64,1152]{1,0:T(8,128)(2,1)S(1)} %pad_maximum_fusion.2), channel_id=1, source_target_pairs={{0,24},{1,25},{2,26},{3,27},{4,28},{5,29},{6,30},{7,31},{8,16},{9,... | collective-permute-start | bytes 442376 | tf_op jit(solution)/shard_map/ppermute | solution.py:651
  22.2 4.6 %collective-permute-start.8 = (bf16[4,64,384]{2,1,0:T(8,128)(2,1)S(1)}, bf16[4,64,384]{2,1,0:T(8,128)(2,1)S(1)}, u32[]{:S(2)}, u32[]{:S(2)}) collective-permute-start(bf16[4,64,384]{2,1,0:T(8,128)(2,1)S(1)} %pad_maximum_fusion.1.refs_4_), channel_id=1, source_target_pairs={{0,2},{1,3},{2,0},{3,1},{4,6},{5,7},{6,4},{7,5},{8,10},{9,11},{10,... | collective-permute-start | bytes 589832 | tf_op jit(solution)/shard_map/ppermute | solution.py:651
  27.9 4.2 %collective-permute-done.8.refs_6_ = bf16[4,64,384]{2,1,0:T(8,128)(2,1)S(1)} collective-permute-done((bf16[4,64,384]{2,1,0:T(8,128)(2,1)S(1)}, bf16[4,64,384]{2,1,0:T(8,128)(2,1)S(1)}, u32[]{:S(2)}, u32[]{:S(2)}) %collective-permute-start.8) | collective-permute-done | bytes 196640 | tf_op jit(solution)/shard_map/ppermute | solution.py:651
  32.1 2.5 %collective-permute-done.9.refs_7_ = bf16[4,64,384]{2,1,0:T(8,128)(2,1)S(1)} collective-permute-done((bf16[4,64,384]{2,1,0:T(8,128)(2,1)S(1)}, bf16[4,64,384]{2,1,0:T(8,128)(2,1)S(1)}, u32[]{:S(2)}, u32[]{:S(2)}) %collective-permute-start.9) | collective-permute-done | bytes 196640 | tf_op jit(solution)/shard_map/ppermute | solution.py:651
  40.5 5.7 %shard_map.439 = (bf16[2048,1536]{1,0:T(8,128)(2,1)S(1)}, bf16[512,2048]{1,0:T(8,128)(2,1)S(1)}, bf16[512,2048]{1,0:T(8,128)(2,1)S(1)}, bf16[512,2048]{1,0:T(8,128)(2,1)S(1)}, bf16[512,1536]{1,0:T(8,128)(2,1)S(1)}) custom-call(s32[4]{0:T(128)S(1)} %and_select_fusion.first_ref, s32[32]{0:T(128)S(1)} %xor_add_fusion.1.refs_0_, f32[4,512]{1,0:T(4,128)S(1)} %copy-done.5, ...), custom_call_target="tpu_custom_call" | custom-call | flops 3221225472 | bytes 16252928 | tf_op jit(solution)/shard_map/pallas_call | solution.py:50
  46.3 12.8 %shard_map.440 = (bf16[1024,512]{1,0:T(8,128)(2,1)S(1)}, f32[8,1024]{1,0:T(8,128)S(1)}) custom-call(s32[4]{0:T(128)S(1)} %and_select_fusion.first_ref, s32[1,1024]{1,0:T(1,128)S(1)} %bitcast.50, bf16[2048,1536]{1,0:T(8,128)(2,1)S(1)} %get-tuple-element.148.qkv_ref.refs_3_, bf16[512,2048]{1,0:T(8,128)(2,1)S(1)} %get-tuple-element.149.vt_ref), custom_call_target="tpu_custom_call" | custom-call | flops 8589934592 | bytes 10485760 | tf_op jit(solution)/shard_map/pallas_call | solution.py:50
  59.2 6.0 %collective-permute-done.16.refs_10_ = bf16[4,64,1152]{2,1,0:T(8,128)(2,1)} collective-permute-done((bf16[4,64,1152]{2,1,0:T(8,128)(2,1)S(1)}, bf16[4,64,1152]{2,1,0:T(8,128)(2,1)}, u32[]{:S(2)}, u32[]{:S(2)}) %collective-permute-start.16) | collective-permute-done | bytes 589856 | tf_op jit(solution)/shard_map/ppermute | solution.py:651
  70.0 21.6 %shard_map.441 = (bf16[1024,512]{1,0:T(8,128)(2,1)}, bf16[1024,512]{1,0:T(8,128)(2,1)S(1)}, f32[1024,512]{1,0:T(8,128)S(1)}, f32[2,512]{1,0:T(2,128)S(1)}, bf16[...) custom-call(s32[32]{0:T(128)S(1)} %xor_add_fusion.1.refs_0_, ...), custom_call_target="tpu_custom_call" | custom-call | flops 14495514624 | bytes 14680064 | tf_op jit(solution)/shard_map/pallas_call | solution.py:50
  91.9 3.5 %shard_map.442 = bf16[16,64,1152]{2,1,0:T(8,128)(2,1)S(1)} custom-call(s32[32]{0:T(128)S(1)} %xor_add_fusion.refs_1_.slots_ref.refs_0_, s32[2]{0:T(128)S(1)} %pad_add_fusion.refs_2_.side_ref.refs_1_, bf16[1024,512]{1,0:T(8,128)(2,1)S(1)} %get-tuple-element.152.refs_3_.refs_0_.refs_6_, bf16[1024,1024]{1,0:T(8,128)(2,1)S(1)} %get-tuple-element.165.refs_1_, ...), custom_call_target="tpu_custom_call" | custom-call | flops 2415919104 | bytes 8388608 | tf_op jit(solution)/shard_map/pallas_call | solution.py:50
  100.6 22.8 %shard_map.443 = (bf16[1536,2048]{1,0:T(8,128)(2,1)S(1)}, bf16[16,64,384]{2,1,0:T(8,128)(2,1)S(1)}, bf16[16,64,384]{2,1,0:T(8,128)(2,1)S(1)}) custom-call(s32[4]{0:T(128)S(1)} %and_select_fusion.first_ref, s32[32]{0:T(128)S(1)} %xor_add_fusion.refs_1_.slots_ref.refs_0_, s32[2]{0:T(128)S(1)} %pad_add_fusion.refs_2_.side_ref.refs_1_, s32[1,1024]{1,0:T(1,128)S(1)} %bitcast.51, ...), custom_call_target="tpu_custom_call" | custom-call | flops 21474836480 | bytes 18874368 | tf_op jit(solution)/shard_map/pallas_call | solution.py:50
  123.4 2.9 %collective-permute-done.24 = bf16[4,64,1152]{2,1,0:T(8,128)(2,1)S(1)} collective-permute-done((bf16[4,64,1152]{2,1,0:T(8,128)(2,1)S(1)}, bf16[4,64,1152]{2,1,0:T(8,128)(2,1)S(1)}, u32[]{:S(2)}, u32[]{:S(2)}) %collective-permute-start.24) | collective-permute-done | bytes 589856 | tf_op jit(solution)/shard_map/ppermute | solution.py:651
  127.1 3.7 %collective-permute-start.26 = (bf16[64,1152]{1,0:T(8,128)(2,1)S(1)}, bf16[64,1152]{1,0:T(8,128)(2,1)S(1)}, u32[]{:S(2)}, u32[]{:S(2)}) collective-permute-start(bf16[64,1152]{1,0:T(8,128)(2,1)S(1)} %get-tuple-element.260), channel_id=1, source_target_pairs={{0,16},{1,17},{2,18},{3,19},{4,20},{5,21},{6,22},{7,23},{8,24},{9,... | collective-permute-start | bytes 442376 | tf_op jit(solution)/shard_map/ppermute | solution.py:651
  132.6 4.2 %collective-permute-start.30 = (bf16[4,64,384]{2,1,0:T(8,128)(2,1)S(1)}, bf16[4,64,384]{2,1,0:T(8,128)(2,1)S(1)}, u32[]{:S(2)}, u32[]{:S(2)}) collective-permute-start(bf16[4,64,384]{2,1,0:T(8,128)(2,1)S(1)} %get-tuple-element.264), channel_id=1, source_target_pairs={{0,2},{1,3},{2,0},{3,1},{4,6},{5,7},{6,4},{7,5},{8,10},{9,11},{10,... | collective-permute-start | bytes 589832 | tf_op jit(solution)/shard_map/ppermute | solution.py:651
  136.8 4.2 %shard_map.444 = (f32[1024,512]{1,0:T(8,128)S(1)}, bf16[1024,512]{1,0:T(8,128)(2,1)S(1)}, f32[2,512]{1,0:T(2,128)S(1)}) custom-call(s32[4]{0:T(128)S(1)} %and_select_fusion.first_ref, f32[4,512]{1,0:T(4,128)S(1)} %copy-done.5, bf16[512,1536]{1,0:T(8,128)(2,1)S(1)} %get-tuple-element.158.w_ref, f32[1024,512]{1,0:T(8,128)S(1)} %get-tuple-element.159.gmid_ref, ...), custom_call_target="tpu_custom_call" | custom-call | flops 3221225472 | bytes 14680064 | tf_op jit(solution)/shard_map/pallas_call | solution.py:50
  142.6 2.4 %collective-permute-done.31 = bf16[4,64,384]{2,1,0:T(8,128)(2,1)S(1)} collective-permute-done((bf16[4,64,384]{2,1,0:T(8,128)(2,1)S(1)}, bf16[4,64,384]{2,1,0:T(8,128)(2,1)S(1)}, u32[]{:S(2)}, u32[]{:S(2)}) %collective-permute-start.31) | collective-permute-done | bytes 196640 | tf_op jit(solution)/shard_map/ppermute | solution.py:651
  145.8 3.5 %collective-permute-start.33 = (bf16[64,384]{1,0:T(8,128)(2,1)S(1)}, bf16[64,384]{1,0:T(8,128)(2,1)S(1)}, u32[]{:S(2)}, u32[]{:S(2)}) collective-permute-start(bf16[64,384]{1,0:T(8,128)(2,1)S(1)} %get-tuple-element.268), channel_id=1, source_target_pairs={{0,16},{1,17},{2,18},{3,19},{4,20},{5,21},{6,22},{7,23},{8,24},{9,... | collective-permute-start | bytes 147464 | tf_op jit(solution)/shard_map/ppermute | solution.py:651
  149.6 2.8 %collective-permute-done.33.refs_6_ = bf16[64,384]{1,0:T(8,128)(2,1)S(1)} collective-permute-done((bf16[64,384]{1,0:T(8,128)(2,1)S(1)}, bf16[64,384]{1,0:T(8,128)(2,1)S(1)}, u32[]{:S(2)}, u32[]{:S(2)}) %collective-permute-start.33) | collective-permute-done | bytes 49184 | tf_op jit(solution)/shard_map/ppermute | solution.py:651
  152.4 2.8 %collective-permute-done.34.refs_7_ = bf16[64,384]{1,0:T(8,128)(2,1)S(1)} collective-permute-done((bf16[64,384]{1,0:T(8,128)(2,1)S(1)}, bf16[64,384]{1,0:T(8,128)(2,1)S(1)}, u32[]{:S(2)}, u32[]{:S(2)}) %collective-permute-start.34) | collective-permute-done | bytes 49184 | tf_op jit(solution)/shard_map/ppermute | solution.py:651
  160.9 3.3 %collective-permute-start.38 = (f32[8,512]{1,0:T(8,128)S(1)}, f32[8,512]{1,0:T(8,128)S(1)}, u32[]{:S(2)}, u32[]{:S(2)}) collective-permute-start(f32[8,512]{1,0:T(8,128)S(1)} %add.243), channel_id=1, source_target_pairs={{0,24},{1,25},{2,26},{3,27},{4,28},{5,29},{6,30},{7,31},{8,16},{9,... | collective-permute-start | bytes 49160 | tf_op jit(solution)/shard_map/ppermute | solution.py:651
  172.3 2.4 %collective-permute-done.41.refs_3_ = f32[8,512]{1,0:T(8,128)S(1)} collective-permute-done((f32[8,512]{1,0:T(8,128)S(1)}, f32[8,512]{1,0:T(8,128)S(1)}, u32[]{:S(2)}, u32[]{:S(2)}) %collective-permute-start.41) | collective-permute-done | bytes 16416 | tf_op jit(solution)/shard_map/ppermute | solution.py:651
  (115 shorter events, 45.9 us)
Async XLA Ops:
  0.7 14.7 %collective-permute-start.3 = (bf16[1024,512]{1,0:T(8,128)(2,1)}, bf16[1024,512]{1,0:T(8,128)(2,1)S(1)}, u32[]{:S(2)}, u32[]{:S(2)}) collective-permute-start(bf16[1024,512]{1,0:T(8,128)(2,1)} %own_far.1), channel_id=1, source_target_pairs={{0,1},{1,2},{2,3},{4,5},{5,6},{6,7},{8,9},{9,10},{10,11},{12,13},{... | collective-permute-start | bytes 3145736 | tf_op jit(solution)/shard_map/ppermute | solution.py:893
  4.1 7.7 %collective-permute-start = (bf16[64,384]{1,0:T(8,128)(2,1)S(1)}, bf16[64,384]{1,0:T(8,128)(2,1)S(1)}, u32[]{:S(2)}, u32[]{:S(2)}) collective-permute-start(bf16[64,384]{1,0:T(8,128)(2,1)S(1)} %pad_maximum_fusion.3), channel_id=1, source_target_pairs={{0,8},{1,9},{2,10},{3,11},{4,12},{5,13},{6,14},{7,15},{8,0},{9,1},... | collective-permute-start | bytes 147464 | tf_op jit(solution)/shard_map/ppermute | solution.py:651
  6.5 6.4 %collective-permute-start.1 = (bf16[64,384]{1,0:T(8,128)(2,1)S(1)}, bf16[64,384]{1,0:T(8,128)(2,1)S(1)}, u32[]{:S(2)}, u32[]{:S(2)}) collective-permute-start(bf16[64,384]{1,0:T(8,128)(2,1)S(1)} %pad_maximum_fusion.3), channel_id=1, source_target_pairs={{0,16},{1,17},{2,18},{3,19},{4,20},{5,21},{6,22},{7,23},{8,24},{9,... | collective-permute-start | bytes 147464 | tf_op jit(solution)/shard_map/ppermute | solution.py:651
  9.1 6.2 %collective-permute-start.2 = (bf16[64,384]{1,0:T(8,128)(2,1)S(1)}, bf16[64,384]{1,0:T(8,128)(2,1)S(1)}, u32[]{:S(2)}, u32[]{:S(2)}) collective-permute-start(bf16[64,384]{1,0:T(8,128)(2,1)S(1)} %pad_maximum_fusion.3), channel_id=1, source_target_pairs={{0,24},{1,25},{2,26},{3,27},{4,28},{5,29},{6,30},{7,31},{8,16},{9,... | collective-permute-start | bytes 147464 | tf_op jit(solution)/shard_map/ppermute | solution.py:651
  15.4 11.4 %collective-permute-start.4 = (bf16[64,1152]{1,0:T(8,128)(2,1)S(1)}, bf16[64,1152]{1,0:T(8,128)(2,1)S(1)}, u32[]{:S(2)}, u32[]{:S(2)}) collective-permute-start(bf16[64,1152]{1,0:T(8,128)(2,1)S(1)} %pad_maximum_fusion.2), channel_id=1, source_target_pairs={{0,8},{1,9},{2,10},{3,11},{4,12},{5,13},{6,14},{7,15},{8,0},{9,1},... | collective-permute-start | bytes 442376 | tf_op jit(solution)/shard_map/ppermute | solution.py:651
  15.5 11.4 %collective-permute-start.5 = (bf16[64,1152]{1,0:T(8,128)(2,1)S(1)}, bf16[64,1152]{1,0:T(8,128)(2,1)S(1)}, u32[]{:S(2)}, u32[]{:S(2)}) collective-permute-start(bf16[64,1152]{1,0:T(8,128)(2,1)S(1)} %pad_maximum_fusion.2), channel_id=1, source_target_pairs={{0,16},{1,17},{2,18},{3,19},{4,20},{5,21},{6,22},{7,23},{8,24},{9,... | collective-permute-start | bytes 442376 | tf_op jit(solution)/shard_map/ppermute | solution.py:651
  17.0 9.9 %collective-permute-start.6 = (bf16[64,1152]{1,0:T(8,128)(2,1)S(1)}, bf16[64,1152]{1,0:T(8,128)(2,1)}, u32[]{:S(2)}, u32[]{:S(2)}) collective-permute-start(bf16[64,1152]{1,0:T(8,128)(2,1)S(1)} %pad_maximum_fusion.2), channel_id=1, source_target_pairs={{0,24},{1,25},{2,26},{3,27},{4,28},{5,29},{6,30},{7,31},{8,16},{9,... | collective-permute-start | bytes 442376 | tf_op jit(solution)/shard_map/ppermute | solution.py:651
  20.7 7.3 %collective-permute-start.7 = (bf16[4,64,384]{2,1,0:T(8,128)(2,1)S(1)}, bf16[4,64,384]{2,1,0:T(8,128)(2,1)S(1)}, u32[]{:S(2)}, u32[]{:S(2)}) collective-permute-start(bf16[4,64,384]{2,1,0:T(8,128)(2,1)S(1)} %pad_maximum_fusion.1.refs_4_), channel_id=1, source_target_pairs={{0,4},{1,5},{2,6},{3,7},{4,0},{5,1},{6,2},{7,3},{8,12},{9,13},{10,... | collective-permute-start | bytes 589832 | tf_op jit(solution)/shard_map/ppermute | solution.py:651
  22.2 9.9 %collective-permute-start.8 = (bf16[4,64,384]{2,1,0:T(8,128)(2,1)S(1)}, bf16[4,64,384]{2,1,0:T(8,128)(2,1)S(1)}, u32[]{:S(2)}, u32[]{:S(2)}) collective-permute-start(bf16[4,64,384]{2,1,0:T(8,128)(2,1)S(1)} %pad_maximum_fusion.1.refs_4_), channel_id=1, source_target_pairs={{0,2},{1,3},{2,0},{3,1},{4,6},{5,7},{6,4},{7,5},{8,10},{9,11},{10,... | collective-permute-start | bytes 589832 | tf_op jit(solution)/shard_map/ppermute | solution.py:651
  26.9 7.8 %collective-permute-start.9 = (bf16[4,64,384]{2,1,0:T(8,128)(2,1)S(1)}, bf16[4,64,384]{2,1,0:T(8,128)(2,1)S(1)}, u32[]{:S(2)}, u32[]{:S(2)}) collective-permute-start(bf16[4,64,384]{2,1,0:T(8,128)(2,1)S(1)} %pad_maximum_fusion.1.refs_4_), channel_id=1, source_target_pairs={{0,6},{1,7},{2,4},{3,5},{4,2},{5,3},{6,0},{7,1},{8,14},{9,15},{10,... | collective-permute-start | bytes 589832 | tf_op jit(solution)/shard_map/ppermute | solution.py:651
  35.7 23.4 %collective-permute-start.14 = (bf16[4,64,1152]{2,1,0:T(8,128)(2,1)S(1)}, bf16[4,64,1152]{2,1,0:T(8,128)(2,1)}, u32[]{:S(2)}, u32[]{:S(2)}) collective-permute-start(bf16[4,64,1152]{2,1,0:T(8,128)(2,1)S(1)} %pad_maximum_fusion.refs_7_), channel_id=1, source_target_pairs={{0,4},{1,5},{2,6},{3,7},{4,0},{5,1},{6,2},{7,3},{8,12},{9,13},{10,... | collective-permute-start | bytes 1769480 | tf_op jit(solution)/shard_map/ppermute | solution.py:651
  37.3 21.9 %collective-permute-start.15 = (bf16[4,64,1152]{2,1,0:T(8,128)(2,1)S(1)}, bf16[4,64,1152]{2,1,0:T(8,128)(2,1)}, u32[]{:S(2)}, u32[]{:S(2)}) collective-permute-start(bf16[4,64,1152]{2,1,0:T(8,128)(2,1)S(1)} %pad_maximum_fusion.refs_7_), channel_id=1, source_target_pairs={{0,2},{1,3},{2,0},{3,1},{4,6},{5,7},{6,4},{7,5},{8,10},{9,11},{10,... | collective-permute-start | bytes 1769480 | tf_op jit(solution)/shard_map/ppermute | solution.py:651
  37.4 27.8 %collective-permute-start.16 = (bf16[4,64,1152]{2,1,0:T(8,128)(2,1)S(1)}, bf16[4,64,1152]{2,1,0:T(8,128)(2,1)}, u32[]{:S(2)}, u32[]{:S(2)}) collective-permute-start(bf16[4,64,1152]{2,1,0:T(8,128)(2,1)S(1)} %pad_maximum_fusion.refs_7_), channel_id=1, source_target_pairs={{0,6},{1,7},{2,4},{3,5},{4,2},{5,3},{6,0},{7,1},{8,14},{9,15},{10,... | collective-permute-start | bytes 1769480 | tf_op jit(solution)/shard_map/ppermute | solution.py:651
  97.0 26.4 %collective-permute-start.22 = (bf16[4,64,1152]{2,1,0:T(8,128)(2,1)S(1)}, bf16[4,64,1152]{2,1,0:T(8,128)(2,1)S(1)}, u32[]{:S(2)}, u32[]{:S(2)}) collective-permute-start(bf16[4,64,1152]{2,1,0:T(8,128)(2,1)S(1)} %get-tuple-element.257), channel_id=1, source_target_pairs={{0,4},{1,5},{2,6},{3,7},{4,0},{5,1},{6,2},{7,3},{8,12},{9,13},{10,... | collective-permute-start | bytes 1769480 | tf_op jit(solution)/shard_map/ppermute | solution.py:651
  98.3 25.1 %collective-permute-start.23 = (bf16[4,64,1152]{2,1,0:T(8,128)(2,1)S(1)}, bf16[4,64,1152]{2,1,0:T(8,128)(2,1)S(1)}, u32[]{:S(2)}, u32[]{:S(2)}) collective-permute-start(bf16[4,64,1152]{2,1,0:T(8,128)(2,1)S(1)} %get-tuple-element.256), channel_id=1, source_target_pairs={{0,2},{1,3},{2,0},{3,1},{4,6},{5,7},{6,4},{7,5},{8,10},{9,11},{10,... | collective-permute-start | bytes 1769480 | tf_op jit(solution)/shard_map/ppermute | solution.py:651
  98.6 27.6 %collective-permute-start.24 = (bf16[4,64,1152]{2,1,0:T(8,128)(2,1)S(1)}, bf16[4,64,1152]{2,1,0:T(8,128)(2,1)S(1)}, u32[]{:S(2)}, u32[]{:S(2)}) collective-permute-start(bf16[4,64,1152]{2,1,0:T(8,128)(2,1)S(1)} %get-tuple-element.255), channel_id=1, source_target_pairs={{0,6},{1,7},{2,4},{3,5},{4,2},{5,3},{6,0},{7,1},{8,14},{9,15},{10,... | collective-permute-start | bytes 1769480 | tf_op jit(solution)/shard_map/ppermute | solution.py:651
  126.6 10.2 %collective-permute-start.25 = (bf16[64,1152]{1,0:T(8,128)(2,1)S(1)}, bf16[64,1152]{1,0:T(8,128)(2,1)S(1)}, u32[]{:S(2)}, u32[]{:S(2)}) collective-permute-start(bf16[64,1152]{1,0:T(8,128)(2,1)S(1)} %get-tuple-element.261), channel_id=1, source_target_pairs={{0,8},{1,9},{2,10},{3,11},{4,12},{5,13},{6,14},{7,15},{8,0},{9,1},... | collective-permute-start | bytes 442376 | tf_op jit(solution)/shard_map/ppermute | solution.py:651
  127.1 14.7 %collective-permute-start.26 = (bf16[64,1152]{1,0:T(8,128)(2,1)S(1)}, bf16[64,1152]{1,0:T(8,128)(2,1)S(1)}, u32[]{:S(2)}, u32[]{:S(2)}) collective-permute-start(bf16[64,1152]{1,0:T(8,128)(2,1)S(1)} %get-tuple-element.260), channel_id=1, source_target_pairs={{0,16},{1,17},{2,18},{3,19},{4,20},{5,21},{6,22},{7,23},{8,24},{9,... | collective-permute-start | bytes 442376 | tf_op jit(solution)/shard_map/ppermute | solution.py:651
  130.8 11.0 %collective-permute-start.27 = (bf16[64,1152]{1,0:T(8,128)(2,1)S(1)}, bf16[64,1152]{1,0:T(8,128)(2,1)S(1)}, u32[]{:S(2)}, u32[]{:S(2)}) collective-permute-start(bf16[64,1152]{1,0:T(8,128)(2,1)S(1)} %get-tuple-element.259), channel_id=1, source_target_pairs={{0,24},{1,25},{2,26},{3,27},{4,28},{5,29},{6,30},{7,31},{8,16},{9,... | collective-permute-start | bytes 442376 | tf_op jit(solution)/shard_map/ppermute | solution.py:651
  131.2 10.5 %collective-permute-start.29 = (bf16[4,64,384]{2,1,0:T(8,128)(2,1)S(1)}, bf16[4,64,384]{2,1,0:T(8,128)(2,1)S(1)}, u32[]{:S(2)}, u32[]{:S(2)}) collective-permute-start(bf16[4,64,384]{2,1,0:T(8,128)(2,1)S(1)} %get-tuple-element.265), channel_id=1, source_target_pairs={{0,4},{1,5},{2,6},{3,7},{4,0},{5,1},{6,2},{7,3},{8,12},{9,13},{10,... | collective-permute-start | bytes 589832 | tf_op jit(solution)/shard_map/ppermute | solution.py:651
  132.6 10.0 %collective-permute-start.30 = (bf16[4,64,384]{2,1,0:T(8,128)(2,1)S(1)}, bf16[4,64,384]{2,1,0:T(8,128)(2,1)S(1)}, u32[]{:S(2)}, u32[]{:S(2)}) collective-permute-start(bf16[4,64,384]{2,1,0:T(8,128)(2,1)S(1)} %get-tuple-element.264), channel_id=1, source_target_pairs={{0,2},{1,3},{2,0},{3,1},{4,6},{5,7},{6,4},{7,5},{8,10},{9,11},{10,... | collective-permute-start | bytes 589832 | tf_op jit(solution)/shard_map/ppermute | solution.py:651
  136.8 8.3 %collective-permute-start.31 = (bf16[4,64,384]{2,1,0:T(8,128)(2,1)S(1)}, bf16[4,64,384]{2,1,0:T(8,128)(2,1)S(1)}, u32[]{:S(2)}, u32[]{:S(2)}) collective-permute-start(bf16[4,64,384]{2,1,0:T(8,128)(2,1)S(1)} %get-tuple-element.263), channel_id=1, source_target_pairs={{0,6},{1,7},{2,4},{3,5},{4,2},{5,3},{6,0},{7,1},{8,14},{9,15},{10,... | collective-permute-start | bytes 589832 | tf_op jit(solution)/shard_map/ppermute | solution.py:651
  145.8 6.7 %collective-permute-start.33 = (bf16[64,384]{1,0:T(8,128)(2,1)S(1)}, bf16[64,384]{1,0:T(8,128)(2,1)S(1)}, u32[]{:S(2)}, u32[]{:S(2)}) collective-permute-start(bf16[64,384]{1,0:T(8,128)(2,1)S(1)} %get-tuple-element.268), channel_id=1, source_target_pairs={{0,16},{1,17},{2,18},{3,19},{4,20},{5,21},{6,22},{7,23},{8,24},{9,... | collective-permute-start | bytes 147464 | tf_op jit(solution)/shard_map/ppermute | solution.py:651
  155.2 14.8 %collective-permute-start.42 = (bf16[1024,512]{1,0:T(8,128)(2,1)S(1)}, bf16[1024,512]{1,0:T(8,128)(2,1)S(1)}, u32[]{:S(2)}, u32[]{:S(2)}) collective-permute-start(bf16[1024,512]{1,0:T(8,128)(2,1)S(1)} %get-tuple-element.200), channel_id=1, source_target_pairs={{1,0},{2,1},{3,2},{5,4},{6,5},{7,6},{9,8},{10,9},{11,10},{13,12},{... | collective-permute-start | bytes 3145736 | tf_op jit(solution)/shard_map/ppermute | solution.py:893
  (30 other events, 252.9 us)

commit v2 on v1

--- a/solution.py
+++ b/solution.py
@@ -492,7 +492,7 @@
     gain, shift = norm_ref[2:3, :], norm_ref[3:4, :]
     ff = up_ref.shape[1]
     d = x_ref.shape[1]
-    wide = min(512, ff)
+    wide = min(1024, ff)
     held = acts[0].shape[1]
     root = 0.7978845608028654
     gain_ref[...] = jnp.zeros_like(gain_ref)
@@ -586,7 +586,7 @@
         scratch,
         flops=2 * n * d * (6 * ff + 3 * d),
         moved=2 * n * 6 * d + 8 * d * ff,
-        room=34,
+        room=36,
     )
 
 

time: 178 us -> 180 us (1.011)
  starting transfers between devices: 52.6 us -> 56 us
    ppermute x41, starting transfers between devices: 48.7 us -> 52.2 us  [swap(): lax.ppermute(value, BOTH, [(i, i ^ bits) for i in range(self.dp * self.mp)])]
  transfers between devices with their start and end apart: 43 -> 43, of which waited for: 22 -> 20; matrix products, arithmetic and copies ran while one was open for 4% -> 4% of each run, Pallas kernels for 29% -> 28%
where the time goes in v2:
time: 180 us
  Pallas kernels  73.7 us (41%)
  starting transfers between devices  56 us (31%)
  waiting for transfers between devices  38.4 us (21%)
  other arithmetic  7.55 us (4%)
  local copies, waits for them, and re-layouts  2.16 us (1%)
  between operations  1.98 us (1%)
    pallas_call x9, Pallas kernels, call(): pl.pallas_call(body, out_shape=outs, in_specs=[pl.BlockSpec(memory_space=...  73.7 us
    ppermute x41, starting transfers between devices, swap(): lax.ppermute(value, BOTH, [(i, i ^ bits) for i in range(self.dp * self.mp)])  52.2 us
    ppermute x41, waiting for transfers between devices, swap(): lax.ppermute(value, BOTH, [(i, i ^ bits) for i in range(self.dp * self.mp)])  38.4 us
    ppermute x2, starting transfers between devices, shifted(): return lax.ppermute(value, 'mp', pairs)  3.84 us
  transfers between devices with their start and end apart: 43, of which 20 were waited for; matrix products, arithmetic and copies ran while one was open for 4% of the time, Pallas kernels for 28%

profile of v2, /device:TPU:0, one launch (start us, length us, event | category | flops | bytes accessed | tf_op | source)
XLA Modules:
  0.0 179.8 jit_solution(17709714004608602674)
XLA Ops:
  0.7 2.6 %collective-permute-start.3 = (bf16[1024,512]{1,0:T(8,128)(2,1)}, bf16[1024,512]{1,0:T(8,128)(2,1)S(1)}, u32[]{:S(2)}, u32[]{:S(2)}) collective-permute-start(bf16[1024,512]{1,0:T(8,128)(2,1)} %own_far.1), channel_id=1, source_target_pairs={{0,1},{1,2},{2,3},{4,5},{5,6},{6,7},{8,9},{9,10},{10,11},{12,13},{... | collective-permute-start | bytes 3145736 | tf_op jit(solution)/shard_map/ppermute | solution.py:893
  4.1 2.5 %collective-permute-start = (bf16[64,384]{1,0:T(8,128)(2,1)S(1)}, bf16[64,384]{1,0:T(8,128)(2,1)S(1)}, u32[]{:S(2)}, u32[]{:S(2)}) collective-permute-start(bf16[64,384]{1,0:T(8,128)(2,1)S(1)} %pad_maximum_fusion.3), channel_id=1, source_target_pairs={{0,8},{1,9},{2,10},{3,11},{4,12},{5,13},{6,14},{7,15},{8,0},{9,1},... | collective-permute-start | bytes 147464 | tf_op jit(solution)/shard_map/ppermute | solution.py:651
  6.5 2.6 %collective-permute-start.1 = (bf16[64,384]{1,0:T(8,128)(2,1)S(1)}, bf16[64,384]{1,0:T(8,128)(2,1)S(1)}, u32[]{:S(2)}, u32[]{:S(2)}) collective-permute-start(bf16[64,384]{1,0:T(8,128)(2,1)S(1)} %pad_maximum_fusion.3), channel_id=1, source_target_pairs={{0,16},{1,17},{2,18},{3,19},{4,20},{5,21},{6,22},{7,23},{8,24},{9,... | collective-permute-start | bytes 147464 | tf_op jit(solution)/shard_map/ppermute | solution.py:651
  12.9 2.4 %collective-permute-done.2 = bf16[64,384]{1,0:T(8,128)(2,1)S(1)} collective-permute-done((bf16[64,384]{1,0:T(8,128)(2,1)S(1)}, bf16[64,384]{1,0:T(8,128)(2,1)S(1)}, u32[]{:S(2)}, u32[]{:S(2)}) %collective-permute-start.2) | collective-permute-done | bytes 49184 | tf_op jit(solution)/shard_map/ppermute | solution.py:651
  17.0 2.9 %collective-permute-start.6 = (bf16[64,1152]{1,0:T(8,128)(2,1)S(1)}, bf16[64,1152]{1,0:T(8,128)(2,1)}, u32[]{:S(2)}, u32[]{:S(2)}) collective-permute-start(bf16[64,1152]{1,0:T(8,128)(2,1)S(1)} %pad_maximum_fusion.2), channel_id=1, source_target_pairs={{0,24},{1,25},{2,26},{3,27},{4,28},{5,29},{6,30},{7,31},{8,16},{9,... | collective-permute-start | bytes 442376 | tf_op jit(solution)/shard_map/ppermute | solution.py:651
  22.2 4.6 %collective-permute-start.8 = (bf16[4,64,384]{2,1,0:T(8,128)(2,1)S(1)}, bf16[4,64,384]{2,1,0:T(8,128)(2,1)S(1)}, u32[]{:S(2)}, u32[]{:S(2)}) collective-permute-start(bf16[4,64,384]{2,1,0:T(8,128)(2,1)S(1)} %pad_maximum_fusion.1.refs_4_), channel_id=1, source_target_pairs={{0,2},{1,3},{2,0},{3,1},{4,6},{5,7},{6,4},{7,5},{8,10},{9,11},{10,... | collective-permute-start | bytes 589832 | tf_op jit(solution)/shard_map/ppermute | solution.py:651
  27.9 4.2 %collective-permute-done.8.refs_6_ = bf16[4,64,384]{2,1,0:T(8,128)(2,1)S(1)} collective-permute-done((bf16[4,64,384]{2,1,0:T(8,128)(2,1)S(1)}, bf16[4,64,384]{2,1,0:T(8,128)(2,1)S(1)}, u32[]{:S(2)}, u32[]{:S(2)}) %collective-permute-start.8) | collective-permute-done | bytes 196640 | tf_op jit(solution)/shard_map/ppermute | solution.py:651
  32.1 2.5 %collective-permute-done.9.refs_7_ = bf16[4,64,384]{2,1,0:T(8,128)(2,1)S(1)} collective-permute-done((bf16[4,64,384]{2,1,0:T(8,128)(2,1)S(1)}, bf16[4,64,384]{2,1,0:T(8,128)(2,1)S(1)}, u32[]{:S(2)}, u32[]{:S(2)}) %collective-permute-start.9) | collective-permute-done | bytes 196640 | tf_op jit(solution)/shard_map/ppermute | solution.py:651
  40.5 5.7 %shard_map.439 = (bf16[2048,1536]{1,0:T(8,128)(2,1)S(1)}, bf16[512,2048]{1,0:T(8,128)(2,1)S(1)}, bf16[512,2048]{1,0:T(8,128)(2,1)S(1)}, bf16[512,2048]{1,0:T(8,128)(2,1)S(1)}, bf16[512,1536]{1,0:T(8,128)(2,1)S(1)}) custom-call(s32[4]{0:T(128)S(1)} %and_select_fusion.first_ref, s32[32]{0:T(128)S(1)} %xor_add_fusion.1.refs_0_, f32[4,512]{1,0:T(4,128)S(1)} %copy-done.5, ...), custom_call_target="tpu_custom_call" | custom-call | flops 3221225472 | bytes 16252928 | tf_op jit(solution)/shard_map/pallas_call | solution.py:50
  46.3 12.8 %shard_map.440 = (bf16[1024,512]{1,0:T(8,128)(2,1)S(1)}, f32[8,1024]{1,0:T(8,128)S(1)}) custom-call(s32[4]{0:T(128)S(1)} %and_select_fusion.first_ref, s32[1,1024]{1,0:T(1,128)S(1)} %bitcast.50, bf16[2048,1536]{1,0:T(8,128)(2,1)S(1)} %get-tuple-element.148.qkv_ref.refs_3_, bf16[512,2048]{1,0:T(8,128)(2,1)S(1)} %get-tuple-element.149.vt_ref), custom_call_target="tpu_custom_call" | custom-call | flops 8589934592 | bytes 10485760 | tf_op jit(solution)/shard_map/pallas_call | solution.py:50
  59.2 6.0 %collective-permute-done.16.refs_10_ = bf16[4,64,1152]{2,1,0:T(8,128)(2,1)} collective-permute-done((bf16[4,64,1152]{2,1,0:T(8,128)(2,1)S(1)}, bf16[4,64,1152]{2,1,0:T(8,128)(2,1)}, u32[]{:S(2)}, u32[]{:S(2)}) %collective-permute-start.16) | collective-permute-done | bytes 589856 | tf_op jit(solution)/shard_map/ppermute | solution.py:651
  70.0 20.8 %shard_map.441 = (bf16[1024,512]{1,0:T(8,128)(2,1)}, bf16[1024,512]{1,0:T(8,128)(2,1)S(1)}, f32[1024,512]{1,0:T(8,128)S(1)}, f32[2,512]{1,0:T(2,128)S(1)}, bf16[...) custom-call(s32[32]{0:T(128)S(1)} %xor_add_fusion.1.refs_0_, ...), custom_call_target="tpu_custom_call" | custom-call | flops 14495514624 | bytes 14680064 | tf_op jit(solution)/shard_map/pallas_call | solution.py:50
  91.1 3.5 %shard_map.442 = bf16[16,64,1152]{2,1,0:T(8,128)(2,1)S(1)} custom-call(s32[32]{0:T(128)S(1)} %xor_add_fusion.refs_1_.slots_ref.refs_0_, s32[2]{0:T(128)S(1)} %pad_add_fusion.refs_2_.side_ref.refs_1_, bf16[1024,512]{1,0:T(8,128)(2,1)S(1)} %get-tuple-element.152.refs_3_.refs_0_.refs_6_, bf16[1024,1024]{1,0:T(8,128)(2,1)S(1)} %get-tuple-element.165.refs_1_, ...), custom_call_target="tpu_custom_call" | custom-call | flops 2415919104 | bytes 8388608 | tf_op jit(solution)/shard_map/pallas_call | solution.py:50
  99.8 22.8 %shard_map.443 = (bf16[1536,2048]{1,0:T(8,128)(2,1)S(1)}, bf16[16,64,384]{2,1,0:T(8,128)(2,1)S(1)}, bf16[16,64,384]{2,1,0:T(8,128)(2,1)S(1)}) custom-call(s32[4]{0:T(128)S(1)} %and_select_fusion.first_ref, s32[32]{0:T(128)S(1)} %xor_add_fusion.refs_1_.slots_ref.refs_0_, s32[2]{0:T(128)S(1)} %pad_add_fusion.refs_2_.side_ref.refs_1_, s32[1,1024]{1,0:T(1,128)S(1)} %bitcast.51, ...), custom_call_target="tpu_custom_call" | custom-call | flops 21474836480 | bytes 18874368 | tf_op jit(solution)/shard_map/pallas_call | solution.py:50
  122.6 2.9 %collective-permute-done.24 = bf16[4,64,1152]{2,1,0:T(8,128)(2,1)S(1)} collective-permute-done((bf16[4,64,1152]{2,1,0:T(8,128)(2,1)S(1)}, bf16[4,64,1152]{2,1,0:T(8,128)(2,1)S(1)}, u32[]{:S(2)}, u32[]{:S(2)}) %collective-permute-start.24) | collective-permute-done | bytes 589856 | tf_op jit(solution)/shard_map/ppermute | solution.py:651
  126.3 3.7 %collective-permute-start.26 = (bf16[64,1152]{1,0:T(8,128)(2,1)S(1)}, bf16[64,1152]{1,0:T(8,128)(2,1)S(1)}, u32[]{:S(2)}, u32[]{:S(2)}) collective-permute-start(bf16[64,1152]{1,0:T(8,128)(2,1)S(1)} %get-tuple-element.260), channel_id=1, source_target_pairs={{0,16},{1,17},{2,18},{3,19},{4,20},{5,21},{6,22},{7,23},{8,24},{9,... | collective-permute-start | bytes 442376 | tf_op jit(solution)/shard_map/ppermute | solution.py:651
  131.8 7.1 %collective-permute-start.30 = (bf16[4,64,384]{2,1,0:T(8,128)(2,1)S(1)}, bf16[4,64,384]{2,1,0:T(8,128)(2,1)S(1)}, u32[]{:S(2)}, u32[]{:S(2)}) collective-permute-start(bf16[4,64,384]{2,1,0:T(8,128)(2,1)S(1)} %get-tuple-element.264), channel_id=1, source_target_pairs={{0,2},{1,3},{2,0},{3,1},{4,6},{5,7},{6,4},{7,5},{8,10},{9,11},{10,... | collective-permute-start | bytes 589832 | tf_op jit(solution)/shard_map/ppermute | solution.py:651
  139.0 4.2 %shard_map.444 = (f32[1024,512]{1,0:T(8,128)S(1)}, bf16[1024,512]{1,0:T(8,128)(2,1)S(1)}, f32[2,512]{1,0:T(2,128)S(1)}) custom-call(s32[4]{0:T(128)S(1)} %and_select_fusion.first_ref, f32[4,512]{1,0:T(4,128)S(1)} %copy-done.5, bf16[512,1536]{1,0:T(8,128)(2,1)S(1)} %get-tuple-element.158.w_ref, f32[1024,512]{1,0:T(8,128)S(1)} %get-tuple-element.159.gmid_ref, ...), custom_call_target="tpu_custom_call" | custom-call | flops 3221225472 | bytes 14680064 | tf_op jit(solution)/shard_map/pallas_call | solution.py:50
  144.7 3.0 %collective-permute-done.31 = bf16[4,64,384]{2,1,0:T(8,128)(2,1)S(1)} collective-permute-done((bf16[4,64,384]{2,1,0:T(8,128)(2,1)S(1)}, bf16[4,64,384]{2,1,0:T(8,128)(2,1)S(1)}, u32[]{:S(2)}, u32[]{:S(2)}) %collective-permute-start.31) | collective-permute-done | bytes 196640 | tf_op jit(solution)/shard_map/ppermute | solution.py:651
  148.4 2.4 %collective-permute-start.33 = (bf16[64,384]{1,0:T(8,128)(2,1)S(1)}, bf16[64,384]{1,0:T(8,128)(2,1)S(1)}, u32[]{:S(2)}, u32[]{:S(2)}) collective-permute-start(bf16[64,384]{1,0:T(8,128)(2,1)S(1)} %get-tuple-element.268), channel_id=1, source_target_pairs={{0,16},{1,17},{2,18},{3,19},{4,20},{5,21},{6,22},{7,23},{8,24},{9,... | collective-permute-start | bytes 147464 | tf_op jit(solution)/shard_map/ppermute | solution.py:651
  153.5 3.2 %collective-permute-done.34.refs_7_ = bf16[64,384]{1,0:T(8,128)(2,1)S(1)} collective-permute-done((bf16[64,384]{1,0:T(8,128)(2,1)S(1)}, bf16[64,384]{1,0:T(8,128)(2,1)S(1)}, u32[]{:S(2)}, u32[]{:S(2)}) %collective-permute-start.34) | collective-permute-done | bytes 49184 | tf_op jit(solution)/shard_map/ppermute | solution.py:651
  163.3 2.4 %collective-permute-start.38 = (f32[8,512]{1,0:T(8,128)S(1)}, f32[8,512]{1,0:T(8,128)S(1)}, u32[]{:S(2)}, u32[]{:S(2)}) collective-permute-start(f32[8,512]{1,0:T(8,128)S(1)} %add.243), channel_id=1, source_target_pairs={{0,24},{1,25},{2,26},{3,27},{4,28},{5,29},{6,30},{7,31},{8,16},{9,... | collective-permute-start | bytes 49160 | tf_op jit(solution)/shard_map/ppermute | solution.py:651
  170.6 2.4 %collective-permute-start.40 = (f32[8,512]{1,0:T(8,128)S(1)}, f32[8,512]{1,0:T(8,128)S(1)}, u32[]{:S(2)}, u32[]{:S(2)}) collective-permute-start(f32[8,512]{1,0:T(8,128)S(1)} %add_add_fusion.refs_0_), channel_id=1, source_target_pairs={{0,4},{1,5},{2,6},{3,7},{4,0},{5,1},{6,2},{7,3},{8,12},{9,13},{10,... | collective-permute-start | bytes 49160 | tf_op jit(solution)/shard_map/ppermute | solution.py:651
  174.9 2.8 %collective-permute-done.41.refs_3_ = f32[8,512]{1,0:T(8,128)S(1)} collective-permute-done((f32[8,512]{1,0:T(8,128)S(1)}, f32[8,512]{1,0:T(8,128)S(1)}, u32[]{:S(2)}, u32[]{:S(2)}) %collective-permute-start.41) | collective-permute-done | bytes 16416 | tf_op jit(solution)/shard_map/ppermute | solution.py:651
  (115 shorter events, 47.7 us)
Async XLA Ops:
  0.7 14.7 %collective-permute-start.3 = (bf16[1024,512]{1,0:T(8,128)(2,1)}, bf16[1024,512]{1,0:T(8,128)(2,1)S(1)}, u32[]{:S(2)}, u32[]{:S(2)}) collective-permute-start(bf16[1024,512]{1,0:T(8,128)(2,1)} %own_far.1), channel_id=1, source_target_pairs={{0,1},{1,2},{2,3},{4,5},{5,6},{6,7},{8,9},{9,10},{10,11},{12,13},{... | collective-permute-start | bytes 3145736 | tf_op jit(solution)/shard_map/ppermute | solution.py:893
  4.1 7.7 %collective-permute-start = (bf16[64,384]{1,0:T(8,128)(2,1)S(1)}, bf16[64,384]{1,0:T(8,128)(2,1)S(1)}, u32[]{:S(2)}, u32[]{:S(2)}) collective-permute-start(bf16[64,384]{1,0:T(8,128)(2,1)S(1)} %pad_maximum_fusion.3), channel_id=1, source_target_pairs={{0,8},{1,9},{2,10},{3,11},{4,12},{5,13},{6,14},{7,15},{8,0},{9,1},... | collective-permute-start | bytes 147464 | tf_op jit(solution)/shard_map/ppermute | solution.py:651
  6.5 6.4 %collective-permute-start.1 = (bf16[64,384]{1,0:T(8,128)(2,1)S(1)}, bf16[64,384]{1,0:T(8,128)(2,1)S(1)}, u32[]{:S(2)}, u32[]{:S(2)}) collective-permute-start(bf16[64,384]{1,0:T(8,128)(2,1)S(1)} %pad_maximum_fusion.3), channel_id=1, source_target_pairs={{0,16},{1,17},{2,18},{3,19},{4,20},{5,21},{6,22},{7,23},{8,24},{9,... | collective-permute-start | bytes 147464 | tf_op jit(solution)/shard_map/ppermute | solution.py:651
  9.1 6.2 %collective-permute-start.2 = (bf16[64,384]{1,0:T(8,128)(2,1)S(1)}, bf16[64,384]{1,0:T(8,128)(2,1)S(1)}, u32[]{:S(2)}, u32[]{:S(2)}) collective-permute-start(bf16[64,384]{1,0:T(8,128)(2,1)S(1)} %pad_maximum_fusion.3), channel_id=1, source_target_pairs={{0,24},{1,25},{2,26},{3,27},{4,28},{5,29},{6,30},{7,31},{8,16},{9,... | collective-permute-start | bytes 147464 | tf_op jit(solution)/shard_map/ppermute | solution.py:651
  15.4 11.4 %collective-permute-start.4 = (bf16[64,1152]{1,0:T(8,128)(2,1)S(1)}, bf16[64,1152]{1,0:T(8,128)(2,1)S(1)}, u32[]{:S(2)}, u32[]{:S(2)}) collective-permute-start(bf16[64,1152]{1,0:T(8,128)(2,1)S(1)} %pad_maximum_fusion.2), channel_id=1, source_target_pairs={{0,8},{1,9},{2,10},{3,11},{4,12},{5,13},{6,14},{7,15},{8,0},{9,1},... | collective-permute-start | bytes 442376 | tf_op jit(solution)/shard_map/ppermute | solution.py:651
  15.5 11.4 %collective-permute-start.5 = (bf16[64,1152]{1,0:T(8,128)(2,1)S(1)}, bf16[64,1152]{1,0:T(8,128)(2,1)S(1)}, u32[]{:S(2)}, u32[]{:S(2)}) collective-permute-start(bf16[64,1152]{1,0:T(8,128)(2,1)S(1)} %pad_maximum_fusion.2), channel_id=1, source_target_pairs={{0,16},{1,17},{2,18},{3,19},{4,20},{5,21},{6,22},{7,23},{8,24},{9,... | collective-permute-start | bytes 442376 | tf_op jit(solution)/shard_map/ppermute | solution.py:651
  17.0 9.9 %collective-permute-start.6 = (bf16[64,1152]{1,0:T(8,128)(2,1)S(1)}, bf16[64,1152]{1,0:T(8,128)(2,1)}, u32[]{:S(2)}, u32[]{:S(2)}) collective-permute-start(bf16[64,1152]{1,0:T(8,128)(2,1)S(1)} %pad_maximum_fusion.2), channel_id=1, source_target_pairs={{0,24},{1,25},{2,26},{3,27},{4,28},{5,29},{6,30},{7,31},{8,16},{9,... | collective-permute-start | bytes 442376 | tf_op jit(solution)/shard_map/ppermute | solution.py:651
  20.7 7.3 %collective-permute-start.7 = (bf16[4,64,384]{2,1,0:T(8,128)(2,1)S(1)}, bf16[4,64,384]{2,1,0:T(8,128)(2,1)S(1)}, u32[]{:S(2)}, u32[]{:S(2)}) collective-permute-start(bf16[4,64,384]{2,1,0:T(8,128)(2,1)S(1)} %pad_maximum_fusion.1.refs_4_), channel_id=1, source_target_pairs={{0,4},{1,5},{2,6},{3,7},{4,0},{5,1},{6,2},{7,3},{8,12},{9,13},{10,... | collective-permute-start | bytes 589832 | tf_op jit(solution)/shard_map/ppermute | solution.py:651
  22.2 9.9 %collective-permute-start.8 = (bf16[4,64,384]{2,1,0:T(8,128)(2,1)S(1)}, bf16[4,64,384]{2,1,0:T(8,128)(2,1)S(1)}, u32[]{:S(2)}, u32[]{:S(2)}) collective-permute-start(bf16[4,64,384]{2,1,0:T(8,128)(2,1)S(1)} %pad_maximum_fusion.1.refs_4_), channel_id=1, source_target_pairs={{0,2},{1,3},{2,0},{3,1},{4,6},{5,7},{6,4},{7,5},{8,10},{9,11},{10,... | collective-permute-start | bytes 589832 | tf_op jit(solution)/shard_map/ppermute | solution.py:651
  26.9 7.8 %collective-permute-start.9 = (bf16[4,64,384]{2,1,0:T(8,128)(2,1)S(1)}, bf16[4,64,384]{2,1,0:T(8,128)(2,1)S(1)}, u32[]{:S(2)}, u32[]{:S(2)}) collective-permute-start(bf16[4,64,384]{2,1,0:T(8,128)(2,1)S(1)} %pad_maximum_fusion.1.refs_4_), channel_id=1, source_target_pairs={{0,6},{1,7},{2,4},{3,5},{4,2},{5,3},{6,0},{7,1},{8,14},{9,15},{10,... | collective-permute-start | bytes 589832 | tf_op jit(solution)/shard_map/ppermute | solution.py:651
  35.7 23.4 %collective-permute-start.14 = (bf16[4,64,1152]{2,1,0:T(8,128)(2,1)S(1)}, bf16[4,64,1152]{2,1,0:T(8,128)(2,1)}, u32[]{:S(2)}, u32[]{:S(2)}) collective-permute-start(bf16[4,64,1152]{2,1,0:T(8,128)(2,1)S(1)} %pad_maximum_fusion.refs_7_), channel_id=1, source_target_pairs={{0,4},{1,5},{2,6},{3,7},{4,0},{5,1},{6,2},{7,3},{8,12},{9,13},{10,... | collective-permute-start | bytes 1769480 | tf_op jit(solution)/shard_map/ppermute | solution.py:651
  37.3 21.9 %collective-permute-start.15 = (bf16[4,64,1152]{2,1,0:T(8,128)(2,1)S(1)}, bf16[4,64,1152]{2,1,0:T(8,128)(2,1)}, u32[]{:S(2)}, u32[]{:S(2)}) collective-permute-start(bf16[4,64,1152]{2,1,0:T(8,128)(2,1)S(1)} %pad_maximum_fusion.refs_7_), channel_id=1, source_target_pairs={{0,2},{1,3},{2,0},{3,1},{4,6},{5,7},{6,4},{7,5},{8,10},{9,11},{10,... | collective-permute-start | bytes 1769480 | tf_op jit(solution)/shard_map/ppermute | solution.py:651
  37.4 27.8 %collective-permute-start.16 = (bf16[4,64,1152]{2,1,0:T(8,128)(2,1)S(1)}, bf16[4,64,1152]{2,1,0:T(8,128)(2,1)}, u32[]{:S(2)}, u32[]{:S(2)}) collective-permute-start(bf16[4,64,1152]{2,1,0:T(8,128)(2,1)S(1)} %pad_maximum_fusion.refs_7_), channel_id=1, source_target_pairs={{0,6},{1,7},{2,4},{3,5},{4,2},{5,3},{6,0},{7,1},{8,14},{9,15},{10,... | collective-permute-start | bytes 1769480 | tf_op jit(solution)/shard_map/ppermute | solution.py:651
  96.2 26.4 %collective-permute-start.22 = (bf16[4,64,1152]{2,1,0:T(8,128)(2,1)S(1)}, bf16[4,64,1152]{2,1,0:T(8,128)(2,1)S(1)}, u32[]{:S(2)}, u32[]{:S(2)}) collective-permute-start(bf16[4,64,1152]{2,1,0:T(8,128)(2,1)S(1)} %get-tuple-element.257), channel_id=1, source_target_pairs={{0,4},{1,5},{2,6},{3,7},{4,0},{5,1},{6,2},{7,3},{8,12},{9,13},{10,... | collective-permute-start | bytes 1769480 | tf_op jit(solution)/shard_map/ppermute | solution.py:651
  97.6 25.0 %collective-permute-start.23 = (bf16[4,64,1152]{2,1,0:T(8,128)(2,1)S(1)}, bf16[4,64,1152]{2,1,0:T(8,128)(2,1)S(1)}, u32[]{:S(2)}, u32[]{:S(2)}) collective-permute-start(bf16[4,64,1152]{2,1,0:T(8,128)(2,1)S(1)} %get-tuple-element.256), channel_id=1, source_target_pairs={{0,2},{1,3},{2,0},{3,1},{4,6},{5,7},{6,4},{7,5},{8,10},{9,11},{10,... | collective-permute-start | bytes 1769480 | tf_op jit(solution)/shard_map/ppermute | solution.py:651
  97.9 27.6 %collective-permute-start.24 = (bf16[4,64,1152]{2,1,0:T(8,128)(2,1)S(1)}, bf16[4,64,1152]{2,1,0:T(8,128)(2,1)S(1)}, u32[]{:S(2)}, u32[]{:S(2)}) collective-permute-start(bf16[4,64,1152]{2,1,0:T(8,128)(2,1)S(1)} %get-tuple-element.255), channel_id=1, source_target_pairs={{0,6},{1,7},{2,4},{3,5},{4,2},{5,3},{6,0},{7,1},{8,14},{9,15},{10,... | collective-permute-start | bytes 1769480 | tf_op jit(solution)/shard_map/ppermute | solution.py:651
  125.8 13.1 %collective-permute-start.25 = (bf16[64,1152]{1,0:T(8,128)(2,1)S(1)}, bf16[64,1152]{1,0:T(8,128)(2,1)S(1)}, u32[]{:S(2)}, u32[]{:S(2)}) collective-permute-start(bf16[64,1152]{1,0:T(8,128)(2,1)S(1)} %get-tuple-element.261), channel_id=1, source_target_pairs={{0,8},{1,9},{2,10},{3,11},{4,12},{5,13},{6,14},{7,15},{8,0},{9,1},... | collective-permute-start | bytes 442376 | tf_op jit(solution)/shard_map/ppermute | solution.py:651
  126.3 16.9 %collective-permute-start.26 = (bf16[64,1152]{1,0:T(8,128)(2,1)S(1)}, bf16[64,1152]{1,0:T(8,128)(2,1)S(1)}, u32[]{:S(2)}, u32[]{:S(2)}) collective-permute-start(bf16[64,1152]{1,0:T(8,128)(2,1)S(1)} %get-tuple-element.260), channel_id=1, source_target_pairs={{0,16},{1,17},{2,18},{3,19},{4,20},{5,21},{6,22},{7,23},{8,24},{9,... | collective-permute-start | bytes 442376 | tf_op jit(solution)/shard_map/ppermute | solution.py:651
  130.0 13.2 %collective-permute-start.27 = (bf16[64,1152]{1,0:T(8,128)(2,1)S(1)}, bf16[64,1152]{1,0:T(8,128)(2,1)S(1)}, u32[]{:S(2)}, u32[]{:S(2)}) collective-permute-start(bf16[64,1152]{1,0:T(8,128)(2,1)S(1)} %get-tuple-element.259), channel_id=1, source_target_pairs={{0,24},{1,25},{2,26},{3,27},{4,28},{5,29},{6,30},{7,31},{8,16},{9,... | collective-permute-start | bytes 442376 | tf_op jit(solution)/shard_map/ppermute | solution.py:651
  130.5 12.7 %collective-permute-start.29 = (bf16[4,64,384]{2,1,0:T(8,128)(2,1)S(1)}, bf16[4,64,384]{2,1,0:T(8,128)(2,1)S(1)}, u32[]{:S(2)}, u32[]{:S(2)}) collective-permute-start(bf16[4,64,384]{2,1,0:T(8,128)(2,1)S(1)} %get-tuple-element.265), channel_id=1, source_target_pairs={{0,4},{1,5},{2,6},{3,7},{4,0},{5,1},{6,2},{7,3},{8,12},{9,13},{10,... | collective-permute-start | bytes 589832 | tf_op jit(solution)/shard_map/ppermute | solution.py:651
  131.8 12.9 %collective-permute-start.30 = (bf16[4,64,384]{2,1,0:T(8,128)(2,1)S(1)}, bf16[4,64,384]{2,1,0:T(8,128)(2,1)S(1)}, u32[]{:S(2)}, u32[]{:S(2)}) collective-permute-start(bf16[4,64,384]{2,1,0:T(8,128)(2,1)S(1)} %get-tuple-element.264), channel_id=1, source_target_pairs={{0,2},{1,3},{2,0},{3,1},{4,6},{5,7},{6,4},{7,5},{8,10},{9,11},{10,... | collective-permute-start | bytes 589832 | tf_op jit(solution)/shard_map/ppermute | solution.py:651
  138.9 8.7 %collective-permute-start.31 = (bf16[4,64,384]{2,1,0:T(8,128)(2,1)S(1)}, bf16[4,64,384]{2,1,0:T(8,128)(2,1)S(1)}, u32[]{:S(2)}, u32[]{:S(2)}) collective-permute-start(bf16[4,64,384]{2,1,0:T(8,128)(2,1)S(1)} %get-tuple-element.263), channel_id=1, source_target_pairs={{0,6},{1,7},{2,4},{3,5},{4,2},{5,3},{6,0},{7,1},{8,14},{9,15},{10,... | collective-permute-start | bytes 589832 | tf_op jit(solution)/shard_map/ppermute | solution.py:651
  156.7 16.3 %collective-permute-start.42 = (bf16[1024,512]{1,0:T(8,128)(2,1)S(1)}, bf16[1024,512]{1,0:T(8,128)(2,1)S(1)}, u32[]{:S(2)}, u32[]{:S(2)}) collective-permute-start(bf16[1024,512]{1,0:T(8,128)(2,1)S(1)} %get-tuple-element.200), channel_id=1, source_target_pairs={{1,0},{2,1},{3,2},{5,4},{6,5},{7,6},{9,8},{10,9},{11,10},{13,12},{... | collective-permute-start | bytes 3145736 | tf_op jit(solution)/shard_map/ppermute | solution.py:893
  161.3 6.1 %collective-permute-start.37 = (f32[8,512]{1,0:T(8,128)S(1)}, f32[8,512]{1,0:T(8,128)S(1)}, u32[]{:S(2)}, u32[]{:S(2)}) collective-permute-start(f32[8,512]{1,0:T(8,128)S(1)} %add.243), channel_id=1, source_target_pairs={{0,16},{1,17},{2,18},{3,19},{4,20},{5,21},{6,22},{7,23},{8,24},{9,... | collective-permute-start | bytes 49160 | tf_op jit(solution)/shard_map/ppermute | solution.py:651
  (30 other events, 258.4 us)
